TPU v7x, 256 devices: a whole 4x4x8 slice. The times are simulated.
256 devices in a mesh: grp: 8 (over z), gx: 8 (over y, core), gy: 4 (over x).
Axes of the slice: x: 4, y: 4, z: 8, core: 2. Of those that a mesh axis runs over, the one named last changes fastest.
Arguments:
- fluid_state: bfloat16 [8, 4, 125, 8, 8, 128], P('grp', None, None, 'gx', 'gy'), may hold values from -6 to 6
- mesh_velocity: bfloat16 [8, 3, 125, 8, 8, 128], P('grp', None, None, 'gx', 'gy'), may hold values from -3 to 3
- metric: float32 [8, 3, 8, 8, 128], P('grp', None, 'gx', 'gy'), may hold values from 0.5 to 2
- wall_face: int32 [65536], P(('grp', 'gx', 'gy')), may hold values from 1 to 510, as said below
- wall_owner: int32 [65536, 1], P(('grp', 'gx', 'gy')), may hold values from 0 to 31; in each aligned block of 256 rows (0 to 255, 256 to 511, ...) at most 16 rows name the same one
- wall_target: int32 [65536], P(('grp', 'gx', 'gy')), may hold values from 0 to 4095
- solid_disp: float32 [8, 81, 131072], P('grp', None, ('gx', 'gy')), may hold values from -6 to 6
- modulus: float32 [8, 131072], P('grp', ('gx', 'gy')), may hold values from 0.5 to 4
- stiffness: float32 [81, 81], replicated, may hold values from -0.011 to 2, as said below
Outputs:
- fluid_next: bfloat16 [8, 4, 125, 8, 8, 128], P('grp', None, None, 'gx', 'gy')
- mesh_motion: bfloat16 [8, 6, 125, 8, 8, 128], P('grp', None, None, 'gx', 'gy')
- solid_next: float32 [8, 81, 131072], P('grp', None, ('gx', 'gy'))
Inputs may be any that keep to these rules, and one draw needn't show every extreme that they name: `wall_face`: within the rows of one device the ids are distinct; ids below 256 are lower z faces, the others upper z faces of element id - 256. Walls lie between neighbouring elements of a device along z: the upper face of an element is listed exactly when the lower face of the next element along z is listed; outer z faces of the grid are never listed. `wall_owner`: the owner is the device of this column (gx * size of gy + gy) in solid group 6 + (g mod 2) for a row of fluid group g. Within the rows of one device at most 16 rows name one column, and some column has exactly 16. `wall_target`: A solid element of the owner's block of 4096. `stiffness`: diagonal entries lie in 1 to 2; the off-diagonal entries of a row sum in magnitude to less than 0.9.
All inputs are finite; a program needn't handle non-finite values.
Results may differ from a plain program's by a relative error of at most 0.001.
Values sent between devices are 32-bit elements; how exact they have to be, the bound alone decides.
A program may use at most 128 MiB of HBM per device.

v0:
```python
import functools
import math

import jax
import jax.numpy as jnp
import numpy as np
from jax import lax
from jax.experimental import pallas as pl
from jax.experimental.pallas import tpu as pltpu
from jax.sharding import PartitionSpec as P

F32 = jnp.float32
BF16 = jnp.bfloat16
I32 = jnp.int32

FLUID = 6
SOLID = 2
LEVELS = 3
GX = 8
GY = 4
COLS = GX * GY
DT = 0.05
NU = 0.02
RELAX = 0.8


def points_5():
    return np.array([-1.0, -math.sqrt(3.0 / 7.0), 0.0, math.sqrt(3.0 / 7.0), 1.0])


def weights_5():
    return np.array([0.1, 49.0 / 90.0, 32.0 / 45.0, 49.0 / 90.0, 0.1])


def lagrange_table(centres, points):
    result = np.ones((len(points), len(centres)))
    for column in range(len(centres)):
        for partner in range(len(centres)):
            if partner != column:
                result[:, column] *= (points - centres[partner]) / (
                    centres[column] - centres[partner]
                )
    return result


def derivative_table():
    pts = points_5()
    n = len(pts)
    w = np.ones(n)
    for c in range(n):
        for p in range(n):
            if p != c:
                w[c] = w[c] / (pts[c] - pts[p])
    d = np.zeros((n, n))
    for r in range(n):
        for c in range(n):
            if r != c:
                d[r, c] = w[c] / w[r] / (pts[r] - pts[c])
        d[r, r] = -np.sum(d[r])
    return d.astype(np.float32).astype(np.float64)


def split_np(x):
    hi = np.asarray(x, np.float32).astype(jnp.bfloat16)
    lo = (np.asarray(x, np.float64) - hi.astype(np.float64)).astype(np.float32).astype(jnp.bfloat16)
    return hi, lo


def build_tables():
    d = derivative_table()
    eye = np.eye(5)
    first = [
        np.kron(np.kron(d, eye), eye),
        np.kron(np.kron(eye, d), eye),
        np.kron(np.kron(eye, eye), d),
    ]
    volume = np.zeros((768, 128))
    for k in range(3):
        volume[128 * k : 128 * k + 125, :125] = first[k]
        volume[384 + 128 * k : 384 + 128 * k + 125, :125] = first[k] @ first[k]
    face_pick = np.zeros((192, 128))
    face_slope = np.zeros((192, 128))
    node = np.arange(125).reshape(5, 5, 5)
    for k in range(3):
        for side in range(2):
            ids = np.take(node, 4 * side, axis=k).reshape(25)
            rows = 64 * k + 32 * side + np.arange(25)
            face_pick[rows, ids] = 1.0
            face_slope[rows, :125] = first[k][ids]
    values = lagrange_table(np.array([-1.0, 0.0, 1.0]), points_5())
    project_one = (values * weights_5()[:, None]).T
    project = np.kron(project_one, project_one).astype(np.float32).astype(np.float64)
    interp = np.kron(values, values).astype(np.float32).astype(np.float64)
    load = np.zeros((32, 96))
    for c in range(3):
        load[9 * c : 9 * c + 9, 32 * c : 32 * c + 25] = project
    blend = np.zeros((768, 128))
    for ch in range(6):
        for nd in range(125):
            ij, k = nd // 5, nd % 5
            for side, scale in ((0, 1.0 - k / 4.0), (1, k / 4.0)):
                base = 64 * side + 32 * (ch // 3) + 9 * (ch % 3)
                blend[128 * ch + nd, base : base + 9] = scale * interp[ij]
    vol_hi, vol_lo = split_np(volume)
    fs_hi, fs_lo = split_np(face_slope)
    load_hi, load_lo = split_np(load)
    blend_hi, blend_lo = split_np(blend)
    return dict(
        volume=np.concatenate([vol_hi, vol_lo], 1),
        slope=np.concatenate([fs_hi, fs_lo], 1),
        pick=face_pick.astype(jnp.bfloat16),
        inject=np.ascontiguousarray(face_pick.T).astype(jnp.bfloat16),
        load=np.concatenate([load_hi, load_lo], 1),
        blend=np.concatenate([blend_hi, blend_lo], 1),
    )


def mm(a, b):
    return jnp.dot(a, b, preferred_element_type=F32)


def mm_nt(a, b):
    return lax.dot_general(a, b, (((1,), (1,)), ((), ())), preferred_element_type=F32)


def mm_full(a, b):
    return jnp.dot(a, b, preferred_element_type=F32, precision=lax.Precision.HIGHEST)


def split(x):
    hi = x.astype(BF16)
    return hi, (x - hi.astype(F32)).astype(BF16)


def iota(shape, axis):
    return lax.broadcasted_iota(I32, shape, axis)


def as_bf16(mask):
    return jnp.where(mask, 1.0, 0.0).astype(BF16)


def table_times(table, hi, lo=None):
    k = table.shape[1] // 2
    out = mm(table, jnp.concatenate([hi, hi], 0))
    if lo is not None:
        out = out + mm(table[:, :k], lo)
    return out


def unpack_nodes(raw, count):
    parts = []
    r, c = iota((256, 256), 0), iota((256, 256), 1)
    y, n = r >> 7, r & 127
    for f in range(count):
        pick = as_bf16((c == 2 * f + 2 * n + y) & (n < 125))
        window = raw[248 * f : 248 * f + 256, :].astype(BF16)
        both = mm(pick, window).astype(BF16)
        parts += [both[0:128, :], both[128:256, :]]
    return jnp.concatenate(parts, 1)


def metric_row(metric, k):
    row = metric[k : k + 1, :]
    return jnp.concatenate([row] * 4, 1)


def face_values(tables, metric, hi, lo):
    pick, slope = tables
    s = mm(pick, hi)
    if lo is not None:
        s = s + mm(pick, lo)
    g = table_times(slope, hi, lo)
    plus, minus, scaled = [], [], []
    for k in range(3):
        m = metric_row(metric, k)
        rows = slice(64 * k, 64 * k + 64)
        mg = m * g[rows]
        a, b = 0.5 * mg, 2.0 * s[rows]
        plus.append(a + b)
        minus.append(a - b)
        scaled.append(mg)
    return plus, minus, s, scaled


def column_blocks(x, y):
    return jnp.concatenate([x[:, 256 * f + 128 * y : 256 * f + 128 * y + 128] for f in range(4)], 1)


def place_blocks(x, y):
    parts = []
    zero = jnp.zeros((x.shape[0], 128), F32)
    for f in range(4):
        pair = [zero, zero]
        pair[y] = x[:, 128 * f : 128 * f + 128]
        parts += pair
    return jnp.concatenate(parts, 1)


def shift_z(x, step):
    blocks = []
    for b in range(x.shape[1] // 128):
        blocks.append(pltpu.roll(x[:, 128 * b : 128 * b + 128], step % 128, 1))
    return jnp.concatenate(blocks, 1)


def local_faces(plus, minus, open_lo, open_hi):
    lo_x, hi_x = minus[0][0:32], -plus[0][32:64]
    in_lo = place_blocks(column_blocks(minus[1][32:64], 0), 1)
    in_hi = place_blocks(column_blocks(plus[1][0:32], 1), 0)
    lo_y, hi_y = minus[1][0:32] - in_lo, in_hi - plus[1][32:64]
    nb_lo = shift_z(minus[2][32:64], 1) * open_lo
    nb_hi = shift_z(plus[2][0:32], -1) * open_hi
    lo_z, hi_z = minus[2][0:32] - nb_lo, nb_hi - plus[2][32:64]
    return [lo_x, hi_x, lo_y, hi_y, lo_z, hi_z]


def send_faces(plus, minus):
    return (
        plus[0][0:32],
        minus[0][32:64],
        column_blocks(plus[1][0:32], 0),
        column_blocks(minus[1][32:64], 1),
    )


def remote_faces(rx_lo, rx_hi, ry_lo, ry_hi):
    return [-rx_lo, rx_hi, place_blocks(-ry_lo, 0), place_blocks(ry_hi, 1)]


def inject_faces(inject, faces):
    hi, lo = split(jnp.concatenate(faces, 0))
    k = hi.shape[0]
    return mm(inject[:, 0:k], hi) + mm(inject[:, 0:k], lo)


def open_rows(meta):
    return (
        jnp.concatenate([meta[2:3, 0:256]] * 4, 1),
        jnp.concatenate([meta[3:4, 0:256]] * 4, 1),
    )


def volume_rate(volume, metric, fields, hi, lo, wm):
    blocks = []
    carrier = [
        fields[:, 256 * k : 256 * k + 256] - wm[:, 256 * k : 256 * k + 256].astype(F32)
        for k in range(3)
    ]
    m = [metric[k : k + 1, :] for k in range(3)]
    flow = [carrier[k] * m[k] for k in range(3)]
    curve = [NU * m[k] * m[k] for k in range(3)]
    part_lo = None if lo is None else lo[:, 768:1024]
    press = table_times(volume[0:384], hi[:, 768:1024], part_lo)
    div = None
    for c in range(3):
        cols = slice(256 * c, 256 * c + 256)
        part_lo = None if lo is None else lo[:, cols]
        der = table_times(volume, hi[:, cols], part_lo)
        rate = -m[c] * press[128 * c : 128 * c + 128]
        for k in range(3):
            rate = rate + curve[k] * der[384 + 128 * k : 512 + 128 * k]
            rate = rate - flow[k] * der[128 * k : 128 * k + 128]
        own = m[c] * der[128 * c : 128 * c + 128]
        div = own if div is None else div + own
        blocks.append(rate)
    blocks.append(-div)
    return jnp.concatenate(blocks, 1)


def wall_meta(face, owner):
    d = as_bf16(iota((32, 256), 0) == owner)
    before = as_bf16(iota((256, 256), 0) < iota((256, 256), 1))
    count = mm(d, before)
    slot = jnp.sum(jnp.where(iota((32, 256), 0) == owner, count, 0.0), 0, keepdims=True).astype(I32)
    hit = as_bf16(iota((512, 256), 0) == face)
    walled = mm_nt(jnp.ones((8, 256), BF16), hit)[0:1, :]
    z = iota((1, 256), 1) & 127
    open_lo = jnp.where(z == 0, 0.0, 1.0 - walled[:, 0:256])
    open_hi = jnp.where(z == 127, 0.0, 1.0 - walled[:, 256:512])
    row0 = (owner * 4 + (slot >> 2)).astype(F32)
    row1 = (slot & 3).astype(F32)
    return jnp.concatenate([row0, row1, open_lo, open_hi, jnp.zeros((4, 256), F32)], 0)


def slot_matrix(meta):
    return as_bf16(iota((128, 256), 0) == meta[0:1, :].astype(I32))


def quarter_mask(meta):
    return (iota((128, 256), 0) >> 5) == meta[1:2, :].astype(I32)


def to_slots(meta, rows):
    hi, lo = split(jnp.where(quarter_mask(meta), rows, 0.0))
    a = slot_matrix(meta)
    return mm_nt(a, hi) + mm_nt(a, lo)


def from_slots(meta, packed):
    hi, lo = split(packed.T)
    a = slot_matrix(meta)
    wide = jnp.where(quarter_mask(meta), mm(hi, a) + mm(lo, a), 0.0)
    return (wide[0:32] + wide[32:64]) + (wide[64:96] + wide[96:128])


def wall_loads(load, pick, metric, s, scaled_z, wm):
    wz = mm(pick[128:192], wm[:, 512:768])
    out = []
    for side, sign in ((0, -1.0), (1, 1.0)):
        g = scaled_z[32 * side : 32 * side + 32]
        v = s[128 + 32 * side : 160 + 32 * side]
        parts = [0.2 * sign * g[:, 0:256], 0.2 * sign * g[:, 256:512]]
        w = wz[32 * side : 32 * side + 32]
        parts.append(
            sign * (0.2 * g[:, 512:768] - v[:, 768:1024] + 0.5 * (v[:, 512:768] - w))
        )
        hi, lo = split(jnp.concatenate(parts, 0))
        out.append(table_times(load, hi, lo))
    return jnp.concatenate(out, 1)


def is_fluid():
    return lax.axis_index("grp") < FLUID


def kernel_1(
    state, speed, metric, face, owner, target, stiff, volume, slope, pick, inject,
    u0_o, wm_o, part_o, meta_o, sxl_o, sxh_o, syl_o, syh_o, tgt_o, pow_o, load_o, top_o,
):
    @pl.when(is_fluid())
    def _():
        u0 = unpack_nodes(state[...].astype(F32), 4)
        wm = unpack_nodes(speed[...].astype(F32), 3)
        u0_o[...] = u0
        wm_o[...] = wm
        meta = wall_meta(face[...], owner[...])
        meta_o[...] = meta
        met = metric[...]
        plus, minus, _, _ = face_values((pick[...], slope[...]), met, u0, None)
        sxl, sxh, syl, syh = send_faces(plus, minus)
        sxl_o[...] = sxl
        sxh_o[...] = sxh
        syl_o[...] = syl
        syh_o[...] = syh
        rate = volume_rate(volume[...], met, u0.astype(F32), u0, None, wm)
        faces = local_faces(plus, minus, *open_rows(meta))
        part_o[...] = rate + inject_faces(inject[...], faces)
        rows = jnp.broadcast_to((target[...] + 1).astype(F32), (128, 256))
        tgt_o[...] = to_slots(meta, rows)

    @pl.when(jnp.logical_not(is_fluid()))
    def _():
        pow_, load, top = solid_tables(stiff[...])
        pow_o[...] = pow_
        load_o[...] = load
        top_o[...] = top


def solid_tables(k):
    r, c = iota((128, 128), 0), iota((128, 128), 1)
    eye = r == c
    diag = jnp.where(eye, k, 0.0)
    col = jnp.sum(diag, 1, keepdims=True)
    row = jnp.sum(diag, 0, keepdims=True)
    one = jnp.where(eye, 1.0, 0.0)
    s = one - RELAX * k / col
    s2 = mm_full(s, s)
    s4 = mm_full(s2, s2)
    t = mm_full(one + s, one + s2) * (RELAX / row)
    sel = jnp.where((c == 3 * (r & 31) + 2) & ((r & 31) < 27), 1.0, 0.0)
    load = mm_full(t, sel.T)
    top = mm_full(sel, load).T
    return s4, load, top


def kernel_2(
    part, rxl, rxh, ryl, ryh, metric, u0, wm, meta_r, face, slope, pick, inject, load,
    disp_any, modulus, pow_, tgt,
    v1_o, sxl_o, sxh_o, syl_o, syh_o, pay_o, base_o, d0_o, inv_o,
    disp, wide, sem,
):
    @pl.when(is_fluid())
    def _():
        gx, gy = lax.axis_index("gx"), lax.axis_index("gy")
        meta = meta_r[...]
        met = metric[...]
        zero = jnp.zeros((), F32)
        faces = remote_faces(
            jnp.where(gx > 0, rxl[...], zero),
            jnp.where(gx < GX - 1, rxh[...], zero),
            jnp.where(gy > 0, ryl[...], zero),
            jnp.where(gy < GY - 1, ryh[...], zero),
        )
        rate = part[...] + inject_faces(inject[...], faces)
        v1 = u0[...].astype(F32) + DT * rate
        v1_o[...] = v1
        hi, lo = split(v1)
        plus, minus, s, scaled = face_values((pick[...], slope[...]), met, hi, lo)
        sxl, sxh, syl, syh = send_faces(plus, minus)
        sxl_o[...] = sxl
        sxh_o[...] = sxh
        syl_o[...] = syl
        syh_o[...] = syh
        loads = wall_loads(load[...], pick[...], met, s, scaled[2], wm[...])
        lh, ll = split(loads)
        hit = as_bf16(iota((512, 256), 0) == face[...])
        rows = mm(lh, hit) + mm(ll, hit)
        pay_o[...] = to_slots(meta, jnp.concatenate([rows] * 4, 0))

    @pl.when(jnp.logical_not(is_fluid()))
    def _():
        copy = pltpu.make_async_copy(disp_any, disp, sem)
        copy.start()
        copy.wait()
        d = disp[...]
        r, c = iota((32, 81), 0), iota((32, 81), 1)
        sel = as_bf16((c == 3 * r + 2) & (r < 27))
        r, c = iota((32, 128), 0), iota((32, 128), 1)
        sel_wide = jnp.where((c == 3 * r + 2) & (r < 27), 1.0, 0.0)
        ph, plo = split(mm_full(sel_wide, pow_[...])[:, 0:81])
        dh, dl = split(d)
        base = mm(ph, dh) + (mm(ph, dl) + mm(plo, dh))
        inv = jnp.broadcast_to(1.0 / modulus[...], (32, 4096))
        base = jnp.where(iota((32, 4096), 0) == 27, inv, base)
        bh, bl = split(base)
        wide[0:32, :] = bh
        wide[32:64, :] = bl
        wide[64:96, :] = mm(sel, dh).astype(BF16)
        wide[96:128, :] = mm(sel, dl).astype(BF16)
        targets = tgt[...].astype(I32) - 1
        lane = iota((384, 128), 1)
        base_a = jnp.zeros((384, 128), F32)
        d0_a = jnp.zeros((384, 128), F32)
        inv_a = jnp.zeros((384, 128), F32)
        for q in range(4):
            column = targets[:, 32 * q : 32 * q + 1]
            got = jnp.zeros((384, 128), F32)
            for part_e in range(4):
                e = iota((384, 1024), 1) + 1024 * part_e
                one = as_bf16(e == column)
                got = got + mm_nt(one, wide[:, 1024 * part_e : 1024 * part_e + 1024])
            both = got + pltpu.roll(got, 96, 1)
            here = (lane >> 5) == q
            shift = 32 * q
            base_q = pltpu.roll(both, shift, 1) if shift else both
            d0_q = pltpu.roll(both, (shift + 64) % 128, 1)
            inv_q = jnp.broadcast_to(both[:, 27:28], (384, 128))
            base_a = jnp.where(here, base_q, base_a)
            d0_a = jnp.where(here, d0_q, d0_a)
            inv_a = jnp.where(here, inv_q, inv_a)
        base_o[...] = base_a
        d0_o[...] = d0_a
        inv_o[...] = inv_a


def kernel_3(
    v1, rxl, rxh, ryl, ryh, metric, u0, wm, meta_r, volume, slope, pick, inject,
    pay, tgt, base, inv, top,
    next_o, row_o,
    stage, gathered,
):
    @pl.when(is_fluid())
    def _():
        gx, gy = lax.axis_index("gx"), lax.axis_index("gy")
        met = metric[...]
        zero = jnp.zeros((), F32)
        fields = v1[...]
        hi, lo = split(fields)
        plus, minus, _, _ = face_values((pick[...], slope[...]), met, hi, lo)
        faces = local_faces(plus, minus, *open_rows(meta_r[...]))
        far = remote_faces(
            jnp.where(gx > 0, rxl[...], zero),
            jnp.where(gx < GX - 1, rxh[...], zero),
            jnp.where(gy > 0, ryl[...], zero),
            jnp.where(gy < GY - 1, ryh[...], zero),
        )
        faces = [a + b for a, b in zip(faces[:4], far)] + faces[4:]
        rate = volume_rate(volume[...], met, fields, hi, lo, wm[...])
        rate = rate + inject_faces(inject[...], faces)
        result = 0.5 * (u0[...].astype(F32) + fields) + (0.5 * DT) * rate
        result = result.astype(BF16)
        stage[...] = jnp.zeros((1000, 128), F32)
        r, c = iota((256, 256), 0), iota((256, 256), 1)
        for f in range(4):
            local_r = r - 2 * f
            put = as_bf16((local_r >= 0) & (local_r < 250) & (c == (local_r >> 1) + 128 * (local_r & 1)))
            block = result[:, 256 * f : 256 * f + 256]
            pair = jnp.concatenate([block[:, 0:128], block[:, 128:256]], 0)
            stage[248 * f : 248 * f + 256, :] = stage[248 * f : 248 * f + 256, :] + mm(put, pair)
        next_o[...] = stage[...].astype(BF16)

    @pl.when(jnp.logical_not(is_fluid()))
    def _():
        next_o[...] = jnp.zeros((1000, 128), BF16)
        loads = pay[...]
        targets = tgt[...]
        turned = targets.T
        lane = iota((384, 128), 1)
        for q in range(4):
            h, l = split(jnp.where((lane >> 5) == q, loads, 0.0))
            gathered[384 * q : 384 * q + 384, 0:128] = h
            gathered[384 * q : 384 * q + 384, 128:256] = l
        row = jnp.concatenate([turned[32 * q : 32 * q + 1, :] for q in range(4)], 1)
        th, tl = split(top[...])
        total = jnp.zeros((384, 128), F32)
        for q in range(4):
            same = as_bf16(targets[:, 32 * q : 32 * q + 1] == row)
            acc = mm(same, gathered[...])
            ah, al = split(acc[:, 0:128] + acc[:, 128:256])
            res = mm(ah, th) + (mm(al, th) + mm(ah, tl))
            total = jnp.where((lane >> 5) == q, res, total)
        row_o[...] = base[...] + inv[...] * total


def kernel_4(
    dn, d0, meta_r, face, wm, blend,
    disp_any, modulus, pow_, load, pay, tgt,
    motion_o, solid_any,
    disp, out, gathered, sem, sem_o,
):
    @pl.when(is_fluid())
    def _():
        out[...] = jnp.zeros((81, 4096), F32)
        copy = pltpu.make_async_copy(out, solid_any, sem_o)
        copy.start()
        meta = meta_r[...]
        a = from_slots(meta, dn[...])
        b = from_slots(meta, d0[...])
        rows = jnp.concatenate([a, a - b], 0)
        hi, lo = split(rows)
        hit = as_bf16(iota((512, 256), 0) == face[...])
        faces = mm_nt(hi, hit) + mm_nt(lo, hit)
        faces = jnp.concatenate([faces[:, 0:256], faces[:, 256:512]], 0)
        hi, lo = split(faces)
        for ch in range(6):
            value = table_times(blend[128 * ch : 128 * ch + 128, :], hi, lo)
            if ch >= 3:
                value = value + wm[:, 256 * (ch - 3) : 256 * (ch - 3) + 256].astype(F32)
            motion_o[:, 256 * ch : 256 * ch + 256] = value.astype(BF16)
        copy.wait()

    @pl.when(jnp.logical_not(is_fluid()))
    def _():
        copy = pltpu.make_async_copy(disp_any, disp, sem)
        copy.start()
        motion_o[...] = jnp.zeros((128, 1536), BF16)
        loads = pay[...]
        turned = tgt[...].T.astype(I32) - 1
        lane = iota((384, 128), 1)
        for q in range(4):
            part = pltpu.roll(loads, (128 - 32 * q) % 128, 1) if q else loads
            part = jnp.where(lane < 32, part, 0.0)
            h, l = split(part)
            gathered[384 * q : 384 * q + 384, :] = jnp.where(
                lane < 32, h.astype(F32), pltpu.roll(l.astype(F32), 32, 1)
            ).astype(BF16)
        th, tl = split(load[...][0:81, :])
        sh, sl = split(pow_[...][0:81, 0:81])
        rows = jnp.concatenate([turned[32 * q : 32 * q + 1, :] for q in range(4)], 1)
        copy.wait()
        fold_r, fold_c = iota((128, 128), 0), iota((128, 128), 1)
        fold = as_bf16((fold_r == (fold_c & 31)) & (fold_c < 64))
        table = (mm(th, fold), mm(tl, fold))
        table = (table[0].astype(BF16), table[1].astype(BF16))
        for part_e in range(16):
            cols = slice(256 * part_e, 256 * part_e + 256)
            one = as_bf16(iota((256, 1536), 0) + 256 * part_e == rows)
            force = mm(one, gathered[...])
            fh, fl = split(force)
            add = mm_nt(table[0], fh) + (mm_nt(table[0], fl) + mm_nt(table[1], fh))
            d = disp[:, cols]
            dh, dl = split(d)
            keep = mm(sh, dh) + (mm(sh, dl) + mm(sl, dh))
            out[:, cols] = keep + add / modulus[:, cols]
        copy = pltpu.make_async_copy(out, solid_any, sem_o)
        copy.start()
        copy.wait()


MESH = pl.DeviceIdType.MESH


def at(grp, gx, gy):
    return dict(device_id=(grp, gx, gy), device_id_type=MESH)


def transfer(
    faces_in, pay_in, faces_out, pay_out, send, recv, psend, precv
):
    grp, gx, gy = lax.axis_index("grp"), lax.axis_index("gx"), lax.axis_index("gy")
    fluid = grp < FLUID
    solid = jnp.logical_not(fluid)
    barrier = pltpu.get_barrier_semaphore()
    column = gx * GY + gy
    has = [gx > 0, gx < GX - 1, gy > 0, gy < GY - 1]
    where = [(grp, gx - 1, gy), (grp, gx + 1, gy), (grp, gx, gy - 1), (grp, gx, gy + 1)]
    owner_group = FLUID + lax.rem(grp, SOLID)

    for k in range(4):
        @pl.when(fluid & has[k])
        def _():
            pl.semaphore_signal(barrier, inc=1, **at(*where[k]))

    @pl.when(solid)
    def _():
        def greet(i, carry):
            g = lax.rem(i, LEVELS) * SOLID + (grp - FLUID)
            c = lax.rem(i // LEVELS + column, COLS)
            pl.semaphore_signal(barrier, inc=1, **at(g, c // GY, lax.rem(c, GY)))
            return carry
        lax.fori_loop(0, LEVELS * COLS, greet, 0)

    @pl.when(fluid)
    def _():
        peers = jnp.int32(COLS)
        for k in range(4):
            peers = peers + jnp.where(has[k], 1, 0)
        pl.semaphore_wait(barrier, peers)

    other = [1, 0, 3, 2]
    copies = []
    for k in range(4):
        copy = pltpu.make_async_remote_copy(
            faces_in[k], faces_out[other[k]], send.at[k], recv.at[other[k]], **at(*where[k])
        )
        copies.append(copy)

        @pl.when(fluid & has[k])
        def _():
            copy.start()

    @pl.when(fluid)
    def _():
        row = (grp // SOLID) * COLS + column

        def push(i, carry):
            o = lax.rem(i + column, COLS)
            pltpu.make_async_remote_copy(
                pay_in.at[o], pay_out.at[row], psend, precv,
                **at(owner_group, o // GY, lax.rem(o, GY)),
            ).start()
            return carry
        lax.fori_loop(0, COLS, push, 0)

    for k in range(4):
        @pl.when(fluid & has[k])
        def _():
            copies[k].wait_send()
            pltpu.make_async_remote_copy(
                faces_in[k], faces_out[k], send.at[k], recv.at[k], **at(*where[k])
            ).wait_recv()

    @pl.when(fluid)
    def _():
        pltpu.make_async_remote_copy(
            pay_in, pay_out.at[pl.ds(0, COLS)], psend, precv, **at(owner_group, gx, gy)
        ).wait_send()

    @pl.when(solid)
    def _():
        pltpu.make_async_remote_copy(
            pay_out, pay_out, psend, precv, **at(0, gx, gy)
        ).wait_recv()


def send_kernel(sxl, sxh, syl, syh, pay, rxl, rxh, ryl, ryh, got, send, recv, psend, precv):
    transfer((sxl, sxh, syl, syh), pay, (rxl, rxh, ryl, ryh), got, send, recv, psend, precv)


def return_kernel(rows, d0, rows_out, d0_out, psend, precv):
    grp, gx, gy = lax.axis_index("grp"), lax.axis_index("gx"), lax.axis_index("gy")
    fluid = grp < FLUID
    solid = jnp.logical_not(fluid)
    barrier = pltpu.get_barrier_semaphore()
    column = gx * GY + gy
    owner_group = FLUID + lax.rem(grp, SOLID)

    @pl.when(fluid)
    def _():
        def greet(i, carry):
            o = lax.rem(i + column, COLS)
            pl.semaphore_signal(barrier, inc=1, **at(owner_group, o // GY, lax.rem(o, GY)))
            return carry
        lax.fori_loop(0, COLS, greet, 0)

    @pl.when(solid)
    def _():
        pl.semaphore_wait(barrier, LEVELS * COLS)

        def push(i, carry):
            level = lax.rem(i, LEVELS)
            g = level * SOLID + (grp - FLUID)
            c = lax.rem(i // LEVELS + column, COLS)
            to = at(g, c // GY, lax.rem(c, GY))
            src = level * COLS + c
            pltpu.make_async_remote_copy(
                rows.at[src], rows_out.at[column], psend.at[0], precv.at[0], **to
            ).start()
            pltpu.make_async_remote_copy(
                d0.at[src], d0_out.at[column], psend.at[1], precv.at[1], **to
            ).start()
            return carry
        lax.fori_loop(0, LEVELS * COLS, push, 0)
        for k, ref in ((0, rows), (1, d0)):
            pltpu.make_async_remote_copy(
                ref, ref, psend.at[k], precv.at[k], **at(0, gx, gy)
            ).wait_send()

    @pl.when(fluid)
    def _():
        for k, ref in ((0, rows_out), (1, d0_out)):
            pltpu.make_async_remote_copy(
                ref, ref, psend.at[k], precv.at[k], **at(owner_group, gx, gy)
            ).wait_recv()


VM = pl.BlockSpec(memory_space=pltpu.VMEM)
ANY = pl.BlockSpec(memory_space=pl.ANY)


def shape(dims, dtype=F32):
    return jax.ShapeDtypeStruct(dims, dtype)


FACE_SHAPES = [shape((32, 1024)), shape((32, 1024)), shape((32, 512)), shape((32, 512))]


def local(
    fluid_state, mesh_velocity, metric, wall_face, wall_owner, wall_target, solid_disp, modulus,
    stiffness,
):
    tab = {k: jnp.asarray(v) for k, v in build_tables().items()}
    state = fluid_state.reshape(1000, 128)
    speed = jnp.pad(mesh_velocity.reshape(750, 128), ((0, 2), (0, 0)))
    met = metric.reshape(3, 256)
    face = wall_face.reshape(1, 256)
    owner = wall_owner.reshape(1, 256)
    target = wall_target.reshape(1, 256)
    disp = solid_disp.reshape(81, 4096)
    mod = modulus.reshape(1, 4096)
    stiff = jnp.pad(stiffness, ((0, 47), (0, 47))) + jnp.asarray(
        np.diag((np.arange(128) >= 81).astype(np.float32))
    )
    params = pltpu.CompilerParams(vmem_limit_bytes=60 * 1024 * 1024)

    u0, wm, part, meta, sxl, sxh, syl, syh, tgt, pow_, load, top = pl.pallas_call(
        kernel_1,
        out_shape=[
            shape((128, 1024), BF16), shape((128, 768), BF16), shape((128, 1024)), shape((8, 256)),
            *FACE_SHAPES, shape((128, 128)), shape((128, 128)), shape((128, 128)),
            shape((128, 128)),
        ],
        in_specs=[VM] * 11,
        out_specs=[VM] * 12,
        compiler_params=params,
        name="fluid_first",
    )(state, speed, met, face, owner, target, stiff, tab["volume"], tab["slope"], tab["pick"],
      tab["inject"])

    def send(cid, faces, pay, name):
        return pl.pallas_call(
            send_kernel,
            out_shape=[*FACE_SHAPES, shape((LEVELS * COLS, 4, 128))],
            in_specs=[ANY] * 5,
            out_specs=[ANY] * 5,
            scratch_shapes=[
                pltpu.SemaphoreType.DMA((4,)), pltpu.SemaphoreType.DMA((4,)),
                pltpu.SemaphoreType.DMA, pltpu.SemaphoreType.DMA,
            ],
            compiler_params=pltpu.CompilerParams(collective_id=cid, has_side_effects=True),
            name=name,
        )(*faces, pay.reshape(COLS, 4, 128))

    rxl, rxh, ryl, ryh, got_t = send(0, (sxl, sxh, syl, syh), tgt, "send_first")
    got_t = got_t.reshape(384, 128)

    v1, sxl, sxh, syl, syh, pay, base, d0, inv = pl.pallas_call(
        kernel_2,
        out_shape=[
            shape((128, 1024)), *FACE_SHAPES, shape((128, 128)), shape((384, 128)),
            shape((384, 128)), shape((384, 128)),
        ],
        in_specs=[VM] * 14 + [ANY] + [VM] * 3,
        out_specs=[VM] * 9,
        scratch_shapes=[
            pltpu.VMEM((81, 4096), F32), pltpu.VMEM((128, 4096), BF16), pltpu.SemaphoreType.DMA,
        ],
        compiler_params=params,
        name="fluid_middle",
    )(part, rxl, rxh, ryl, ryh, met, u0, wm, meta, face, tab["slope"], tab["pick"],
      tab["inject"], tab["load"], disp, mod, pow_, got_t)

    rxl, rxh, ryl, ryh, got_p = send(1, (sxl, sxh, syl, syh), pay, "send_second")
    got_p = got_p.reshape(384, 128)

    fluid_next, rows = pl.pallas_call(
        kernel_3,
        out_shape=[shape((1000, 128), BF16), shape((384, 128))],
        in_specs=[VM] * 18,
        out_specs=[VM] * 2,
        scratch_shapes=[pltpu.VMEM((1000, 128), F32), pltpu.VMEM((1536, 256), BF16)],
        compiler_params=params,
        name="fluid_last",
    )(v1, rxl, rxh, ryl, ryh, met, u0, wm, meta, tab["volume"], tab["slope"], tab["pick"],
      tab["inject"], got_p, got_t, base, inv, top)

    back, back0 = pl.pallas_call(
        return_kernel,
        out_shape=[shape((COLS, 4, 128))] * 2,
        in_specs=[ANY] * 2,
        out_specs=[ANY] * 2,
        scratch_shapes=[pltpu.SemaphoreType.DMA((2,)), pltpu.SemaphoreType.DMA((2,))],
        compiler_params=pltpu.CompilerParams(collective_id=2, has_side_effects=True),
        name="send_back",
    )(rows.reshape(LEVELS * COLS, 4, 128), d0.reshape(LEVELS * COLS, 4, 128))

    motion, solid_next = pl.pallas_call(
        kernel_4,
        out_shape=[shape((128, 1536), BF16), shape((81, 4096))],
        in_specs=[VM] * 6 + [ANY] + [VM] * 5,
        out_specs=[VM, ANY],
        scratch_shapes=[
            pltpu.VMEM((81, 4096), F32), pltpu.VMEM((81, 4096), F32), pltpu.VMEM((1536, 128), BF16),
            pltpu.SemaphoreType.DMA, pltpu.SemaphoreType.DMA,
        ],
        compiler_params=params,
        name="final",
    )(back.reshape(128, 128), back0.reshape(128, 128), meta, face, wm, tab["blend"],
      disp, mod, pow_, load, got_p, got_t)

    motion = motion[0:125].reshape(125, 6, 2, 128).transpose(1, 0, 2, 3)
    return (
        fluid_next.reshape(1, 4, 125, 1, 2, 128),
        motion.reshape(1, 6, 125, 1, 2, 128),
        solid_next.reshape(1, 81, 4096),
    )


def solution(mesh):
    in_specs = (
        P("grp", None, None, "gx", "gy", None),
        P("grp", None, None, "gx", "gy", None),
        P("grp", None, "gx", "gy", None),
        P(("grp", "gx", "gy")),
        P(("grp", "gx", "gy"), None),
        P(("grp", "gx", "gy")),
        P("grp", None, ("gx", "gy")),
        P("grp", ("gx", "gy")),
        P(),
    )
    out_specs = (
        P("grp", None, None, "gx", "gy", None),
        P("grp", None, None, "gx", "gy", None),
        P("grp", None, ("gx", "gy")),
    )
    return jax.shard_map(local, mesh=mesh, in_specs=in_specs, out_specs=out_specs, check_vma=False)
```

profile of v0, /device:TPU:1, one launch (start us, length us, event | category | flops | bytes accessed | tf_op | source)
XLA Modules:
  0.0 84.7 jit_solution(3692825504850585104)
XLA Ops:
  0.6 0.0 copy-start.1
  0.6 1.4 %copy.29 = f32[1,3,2,128]{3,1,2,0:T(4,128)} copy(f32[1,3,2,128]{3,2,1,0:T(2,128)} %bitcast.53) | data formatting | bytes 6144
  2.0 1.5 %pad_add_fusion.stiff = f32[128,128]{1,0:T(8,128)} fusion(f32[128,128]{1,0:T(8,128)} %constant.25.clone, f32[81,81]{1,0:T(8,128)} %param.24), kind=kLoop, calls=%fused_computation.2 | loop fusion | flops 16384 | bytes 157316 | tf_op jit(solution)/shard_map/add | solution.py:742
  3.5 1.2 %reshape.64 = bf16[750,128]{1,0:T(8,128)(2,1)S(1)} reshape(bf16[1,3,125,1,2,128]{5,4,3,2,1,0:T(2,128)(2,1)} %param.17) | data formatting | bytes 384000 | tf_op jit(solution)/shard_map/reshape | solution.py:735
  4.7 0.7 pad.8.speed
  5.4 3.8 %fluid_first.1 = (bf16[128,1024]{1,0:T(8,128)(2,1)}, bf16[128,768]{1,0:T(8,128)(2,1)}, f32[128,1024]{1,0:T(8,128)}, f32[8,256]{1,0:T(8,128)}, f32[32,1024]{1,0:T...) custom-call(bf16[1000,128]{1,0:T(8,128)(2,1)} %bitcast.40, ...), custom_call_target="tpu_custom_call" | custom-call | tf_op jit(solution)/shard_map/fluid_first/pallas_call | solution.py:747
  9.2 17.5 %send_first.1 = (f32[32,1024]{1,0:T(8,128)}, f32[32,1024]{1,0:T(8,128)}, f32[32,512]{1,0:T(8,128)}, f32[32,512]{1,0:T(8,128)}, f32[96,4,128]{2,1,0:T(4,128)}) custom-call(f32[32,1024]{1,0:T(8,128)} %get-tuple-element.41.sxl, f32[32,1024]{1,0:T(8,128)} %get-tuple-element.42.sxh, f32[32,512]{1,0:T(8,128)} %get-tuple-element.43.syl, ...), custom_call_target="tpu_custom_call" | custom-call | tf_op jit(solution)/shard_map/send_first/pallas_call | solution.py:762
  26.7 0.0 copy-done.1
  26.7 2.0 %copy.27 = f32[1,81,4096]{2,1,0:T(8,128)} copy(f32[1,81,4096]{2,0,1:T(1,128)S(1)} %copy-done.1) | data formatting | bytes 2654208
  28.7 4.2 %fluid_middle.1 = (f32[128,1024]{1,0:T(8,128)}, f32[32,1024]{1,0:T(8,128)}, f32[32,1024]{1,0:T(8,128)}, f32[32,512]{1,0:T(8,128)}, f32[32,512]{1,0:T(8,128)}, /*...) custom-call(f32[128,1024]{1,0:T(8,128)} %get-tuple-element.40.part, ...), custom_call_target="tpu_custom_call" | custom-call | tf_op jit(solution)/shard_map/fluid_middle/pallas_call | solution.py:778
  32.9 21.3 %send_second.1 = (f32[32,1024]{1,0:T(8,128)}, f32[32,1024]{1,0:T(8,128)}, f32[32,512]{1,0:T(8,128)}, f32[32,512]{1,0:T(8,128)}, f32[96,4,128]{2,1,0:T(4,128)}) custom-call(f32[32,1024]{1,0:T(8,128)} %get-tuple-element.56.sxl, f32[32,1024]{1,0:T(8,128)} %get-tuple-element.57.sxh, f32[32,512]{1,0:T(8,128)} %get-tuple-element.58.syl, ...), custom_call_target="tpu_custom_call" | custom-call | tf_op jit(solution)/shard_map/send_second/pallas_call | solution.py:762
  54.2 4.6 %fluid_last.1 = (bf16[1000,128]{1,0:T(8,128)(2,1)}, f32[384,128]{1,0:T(8,128)}) custom-call(f32[128,1024]{1,0:T(8,128)} %get-tuple-element.55.v1, f32[32,1024]{1,0:T(8,128)} %get-tuple-element.61.rxl, f32[32,1024]{1,0:T(8,128)} %get-tuple-element.62.rxh, f32[32,512]{1,0:T(8,128)} %get-tuple-element.63.ryl, f32[32,512]{1,0:T(8,128)} %get-tuple-element.64.ryh, ...), custom_call_target="tpu_custom_call" | custom-call | tf_op jit(solution)/shard_map/fluid_last/pallas_call | solution.py:797
  58.8 16.8 %send_back.1 = (f32[32,4,128]{2,1,0:T(4,128)}, f32[32,4,128]{2,1,0:T(4,128)}) custom-call(f32[96,4,128]{2,1,0:T(4,128)} %bitcast.42, f32[96,4,128]{2,1,0:T(4,128)} %bitcast.41), custom_call_target="tpu_custom_call" | custom-call | tf_op jit(solution)/shard_map/send_back/pallas_call | solution.py:808
  75.6 4.0 %final.1 = (bf16[128,1536]{1,0:T(8,128)(2,1)}, f32[81,4096]{1,0:T(8,128)}) custom-call(f32[128,128]{1,0:T(8,128)} %bitcast.48, f32[128,128]{1,0:T(8,128)} %bitcast.49, f32[8,256]{1,0:T(8,128)} %get-tuple-element.52.meta_r, s32[1,256]{1,0:T(1,128)} %bitcast.52, bf16[128,768]{1,0:T(8,128)(2,1)} %get-tuple-element.51.wm, ...), custom_call_target="tpu_custom_call" | custom-call | tf_op jit(solution)/shard_map/final/pallas_call | solution.py:818
  79.6 0.0 copy-start
  79.7 1.6 %reshape.79 = bf16[125,6,2,128]{3,2,1,0:T(2,128)(2,1)S(1)} reshape(bf16[125,1536]{1,0:T(8,128)(2,1)} %bitcast.38) | data formatting | bytes 768000 | tf_op jit(solution)/shard_map/reshape | solution.py:832
  81.3 1.0 %copy.28 = bf16[125,6,2,128]{3,2,0,1:T(2,128)(2,1)} copy(bf16[125,6,2,128]{3,2,1,0:T(2,128)(2,1)S(1)} %reshape.79) | data formatting | bytes 768000 | tf_op jit(solution)/shard_map/reshape | solution.py:832
  82.3 0.0 copy-done
  82.3 2.4 %copy.21 = f32[1,81,4096]{2,0,1:T(1,128)} copy(f32[1,81,4096]{2,1,0:T(8,128)S(1)} %bitcast.35) | data formatting | bytes 2654208
Async XLA Ops:
  0.6 26.1 %copy-start.1 = (f32[1,81,4096]{2,0,1:T(1,128)S(1)}, f32[1,81,4096]{2,0,1:T(1,128)}, u32[]{:S(2)}) copy-start(f32[1,81,4096]{2,0,1:T(1,128)} %param.22) | copy-start | bytes 3981316
  79.6 2.7 %copy-start = (f32[81,4096]{1,0:T(8,128)S(1)}, f32[81,4096]{1,0:T(8,128)}, u32[]{:S(2)}) copy-start(f32[81,4096]{1,0:T(8,128)} %get-tuple-element.76) | copy-start | bytes 3981316
where the time goes:
time: 86.3 us; the launch traced here: 84.7 us
  Pallas kernels  72.2 us (84%)
  local copies, waits for them, and re-layouts  10.3 us (12%)
  other arithmetic  1.48 us (2%)
    pallas_call x2, Pallas kernels, send(): pl.pallas_call(send_kernel, out_shape=[*FACE_SHAPES, shape((LEVELS * COLS...  38.8 us
    pallas_call x1, Pallas kernels, local(): pl.pallas_call(return_kernel, out_shape=[shape((COLS, 4, 128))] * 2, in_s...  16.8 us
    unnamed x7, local copies, waits for them, and re-layouts  5.8 us
    pallas_call x1, Pallas kernels, local(): pl.pallas_call(kernel_3, out_shape=[shape((1000, 128), BF16), shape((384,...  4.6 us
    pallas_call x1, Pallas kernels, local(): pl.pallas_call(kernel_2, out_shape=[shape((128, 1024)), *FACE_SHAPES, sha...  4.17 us
    pallas_call x1, Pallas kernels, local(): pl.pallas_call(kernel_4, out_shape=[shape((128, 1536), BF16), shape((81,...  4.05 us
    pallas_call x1, Pallas kernels, local(): pl.pallas_call(kernel_1, out_shape=[shape((128, 1024), BF16), shape((128,...  3.76 us
    reshape x2, local copies, waits for them, and re-layouts, local(): motion = motion[0:125].reshape(125, 6, 2, 128).transpose(1, 0, 2, 3)  2.63 us

commit v1 on v0

v1 whole, which is shorter than its diff:
```python
import functools
import math

import jax
import jax.numpy as jnp
import numpy as np
from jax import lax
from jax.experimental import pallas as pl
from jax.experimental.pallas import tpu as pltpu
from jax.sharding import PartitionSpec as P

F32 = jnp.float32
BF16 = jnp.bfloat16
I32 = jnp.int32

FLUID = 6
SOLID = 2
LEVELS = 3
GX = 8
GY = 4
COLS = GX * GY
DT = 0.05
NU = 0.02
RELAX = 0.8


def points_5():
    return np.array([-1.0, -math.sqrt(3.0 / 7.0), 0.0, math.sqrt(3.0 / 7.0), 1.0])


def weights_5():
    return np.array([0.1, 49.0 / 90.0, 32.0 / 45.0, 49.0 / 90.0, 0.1])


def lagrange_table(centres, points):
    result = np.ones((len(points), len(centres)))
    for column in range(len(centres)):
        for partner in range(len(centres)):
            if partner != column:
                result[:, column] *= (points - centres[partner]) / (
                    centres[column] - centres[partner]
                )
    return result


def derivative_table():
    pts = points_5()
    n = len(pts)
    w = np.ones(n)
    for c in range(n):
        for p in range(n):
            if p != c:
                w[c] = w[c] / (pts[c] - pts[p])
    d = np.zeros((n, n))
    for r in range(n):
        for c in range(n):
            if r != c:
                d[r, c] = w[c] / w[r] / (pts[r] - pts[c])
        d[r, r] = -np.sum(d[r])
    return d.astype(np.float32).astype(np.float64)


def split_np(x):
    hi = np.asarray(x, np.float32).astype(jnp.bfloat16)
    lo = (np.asarray(x, np.float64) - hi.astype(np.float64)).astype(np.float32).astype(jnp.bfloat16)
    return hi, lo


def build_tables():
    d = derivative_table()
    eye = np.eye(5)
    first = [
        np.kron(np.kron(d, eye), eye),
        np.kron(np.kron(eye, d), eye),
        np.kron(np.kron(eye, eye), d),
    ]
    volume = np.zeros((768, 128))
    for k in range(3):
        volume[128 * k : 128 * k + 125, :125] = first[k]
        volume[384 + 128 * k : 384 + 128 * k + 125, :125] = first[k] @ first[k]
    face_pick = np.zeros((192, 128))
    face_slope = np.zeros((192, 128))
    node = np.arange(125).reshape(5, 5, 5)
    for k in range(3):
        for side in range(2):
            ids = np.take(node, 4 * side, axis=k).reshape(25)
            rows = 64 * k + 32 * side + np.arange(25)
            face_pick[rows, ids] = 1.0
            face_slope[rows, :125] = first[k][ids]
    values = lagrange_table(np.array([-1.0, 0.0, 1.0]), points_5())
    project_one = (values * weights_5()[:, None]).T
    project = np.kron(project_one, project_one).astype(np.float32).astype(np.float64)
    interp = np.kron(values, values).astype(np.float32).astype(np.float64)
    load = np.zeros((32, 96))
    for c in range(3):
        load[9 * c : 9 * c + 9, 32 * c : 32 * c + 25] = project
    blend = np.zeros((768, 128))
    for ch in range(6):
        for nd in range(125):
            ij, k = nd // 5, nd % 5
            for side, scale in ((0, 1.0 - k / 4.0), (1, k / 4.0)):
                base = 64 * side + 32 * (ch // 3) + 9 * (ch % 3)
                blend[128 * ch + nd, base : base + 9] = scale * interp[ij]
    vol_hi, vol_lo = split_np(volume)
    fs_hi, fs_lo = split_np(face_slope)
    load_hi, load_lo = split_np(load)
    blend_hi, blend_lo = split_np(blend)
    return dict(
        volume=np.concatenate([vol_hi, vol_lo], 1),
        slope=np.concatenate([fs_hi, fs_lo], 1),
        pick=face_pick.astype(jnp.bfloat16),
        inject=np.ascontiguousarray(face_pick.T).astype(jnp.bfloat16),
        load=np.concatenate([load_hi, load_lo], 1),
        blend=np.concatenate([blend_hi, blend_lo], 1),
    )


def mm(a, b):
    return jnp.dot(a, b, preferred_element_type=F32)


def mm_nt(a, b):
    return lax.dot_general(a, b, (((1,), (1,)), ((), ())), preferred_element_type=F32)


def mm_full(a, b):
    return jnp.dot(a, b, preferred_element_type=F32, precision=lax.Precision.HIGHEST)


def split(x):
    hi = x.astype(BF16)
    return hi, (x - hi.astype(F32)).astype(BF16)


def iota(shape, axis):
    return lax.broadcasted_iota(I32, shape, axis)


def as_bf16(mask):
    return jnp.where(mask, 1.0, 0.0).astype(BF16)


def table_times(table, hi, lo=None):
    k = table.shape[1] // 2
    out = mm(table, jnp.concatenate([hi, hi], 0))
    if lo is not None:
        out = out + mm(table[:, :k], lo)
    return out


def unpack_nodes(raw, count, stride):
    parts = []
    r, c = iota((256, 256), 0), iota((256, 256), 1)
    y, n = r >> 7, r & 127
    for f in range(count):
        start = stride * f // 8 * 8
        pick = as_bf16((c == stride * f - start + 2 * n + y) & (n < 125))
        window = raw[start : start + 256, :].astype(BF16)
        both = mm(pick, window).astype(BF16)
        parts += [both[0:128, :], both[128:256, :]]
    return jnp.concatenate(parts, 1)


def metric_row(metric, k):
    row = metric[k : k + 1, :]
    return jnp.concatenate([row] * 4, 1)


def face_values(tables, metric, hi, lo):
    pick, slope = tables
    s = mm(pick, hi)
    if lo is not None:
        s = s + mm(pick, lo)
    g = table_times(slope, hi, lo)
    plus, minus, scaled = [], [], []
    for k in range(3):
        m = metric_row(metric, k)
        rows = slice(64 * k, 64 * k + 64)
        mg = m * g[rows]
        a, b = 0.5 * mg, 2.0 * s[rows]
        plus.append(a + b)
        minus.append(a - b)
        scaled.append(mg)
    return plus, minus, s, scaled


def column_blocks(x, y):
    return jnp.concatenate([x[:, 256 * f + 128 * y : 256 * f + 128 * y + 128] for f in range(4)], 1)


def place_blocks(x, y):
    parts = []
    zero = jnp.zeros((x.shape[0], 128), F32)
    for f in range(4):
        pair = [zero, zero]
        pair[y] = x[:, 128 * f : 128 * f + 128]
        parts += pair
    return jnp.concatenate(parts, 1)


def shift_z(x, step):
    blocks = []
    for b in range(x.shape[1] // 128):
        blocks.append(pltpu.roll(x[:, 128 * b : 128 * b + 128], step % 128, 1))
    return jnp.concatenate(blocks, 1)


def local_faces(plus, minus, open_lo, open_hi):
    lo_x, hi_x = minus[0][0:32], -plus[0][32:64]
    in_lo = place_blocks(column_blocks(minus[1][32:64], 0), 1)
    in_hi = place_blocks(column_blocks(plus[1][0:32], 1), 0)
    lo_y, hi_y = minus[1][0:32] - in_lo, in_hi - plus[1][32:64]
    nb_lo = shift_z(minus[2][32:64], 1) * open_lo
    nb_hi = shift_z(plus[2][0:32], -1) * open_hi
    lo_z, hi_z = minus[2][0:32] - nb_lo, nb_hi - plus[2][32:64]
    return [lo_x, hi_x, lo_y, hi_y, lo_z, hi_z]


def send_faces(plus, minus):
    return (
        plus[0][0:32],
        minus[0][32:64],
        column_blocks(plus[1][0:32], 0),
        column_blocks(minus[1][32:64], 1),
    )


def remote_faces(rx_lo, rx_hi, ry_lo, ry_hi):
    return [-rx_lo, rx_hi, place_blocks(-ry_lo, 0), place_blocks(ry_hi, 1)]


def inject_faces(inject, faces):
    hi, lo = split(jnp.concatenate(faces, 0))
    k = hi.shape[0]
    return mm(inject[:, 0:k], hi) + mm(inject[:, 0:k], lo)


def flat_metric(metric):
    return jnp.concatenate([metric[:, 0, :], metric[:, 1, :]], 1)


def open_rows(meta):
    return (
        jnp.concatenate([meta[2:3, 0:256]] * 4, 1),
        jnp.concatenate([meta[3:4, 0:256]] * 4, 1),
    )


def volume_rate(volume, metric, fields, hi, lo, wm):
    blocks = []
    carrier = [
        fields[:, 256 * k : 256 * k + 256] - wm[:, 256 * k : 256 * k + 256].astype(F32)
        for k in range(3)
    ]
    m = [metric[k : k + 1, :] for k in range(3)]
    flow = [carrier[k] * m[k] for k in range(3)]
    curve = [NU * m[k] * m[k] for k in range(3)]
    part_lo = None if lo is None else lo[:, 768:1024]
    press = table_times(volume[0:384], hi[:, 768:1024], part_lo)
    div = None
    for c in range(3):
        cols = slice(256 * c, 256 * c + 256)
        part_lo = None if lo is None else lo[:, cols]
        der = table_times(volume, hi[:, cols], part_lo)
        rate = -m[c] * press[128 * c : 128 * c + 128]
        for k in range(3):
            rate = rate + curve[k] * der[384 + 128 * k : 512 + 128 * k]
            rate = rate - flow[k] * der[128 * k : 128 * k + 128]
        own = m[c] * der[128 * c : 128 * c + 128]
        div = own if div is None else div + own
        blocks.append(rate)
    blocks.append(-div)
    return jnp.concatenate(blocks, 1)


def wall_meta(face, owner):
    d = as_bf16(iota((32, 256), 0) == owner)
    before = as_bf16(iota((256, 256), 0) < iota((256, 256), 1))
    count = mm(d, before)
    slot = jnp.sum(jnp.where(iota((32, 256), 0) == owner, count, 0.0), 0, keepdims=True).astype(I32)
    hit = as_bf16(iota((512, 256), 0) == face)
    walled = mm_nt(jnp.ones((8, 256), BF16), hit)[0:1, :]
    z = iota((1, 256), 1) & 127
    open_lo = jnp.where(z == 0, 0.0, 1.0 - walled[:, 0:256])
    open_hi = jnp.where(z == 127, 0.0, 1.0 - walled[:, 256:512])
    row0 = (owner * 4 + (slot >> 2)).astype(F32)
    row1 = (slot & 3).astype(F32)
    return jnp.concatenate([row0, row1, open_lo, open_hi, jnp.zeros((4, 256), F32)], 0)


def slot_matrix(meta):
    return as_bf16(iota((128, 256), 0) == meta[0:1, :].astype(I32))


def quarter_mask(meta):
    return (iota((128, 256), 0) >> 5) == meta[1:2, :].astype(I32)


def to_slots(meta, rows):
    hi, lo = split(jnp.where(quarter_mask(meta), rows, 0.0))
    a = slot_matrix(meta)
    return mm_nt(a, hi) + mm_nt(a, lo)


def from_slots(meta, packed):
    hi, lo = split(packed.T)
    a = slot_matrix(meta)
    wide = jnp.where(quarter_mask(meta), mm(hi, a) + mm(lo, a), 0.0)
    return (wide[0:32] + wide[32:64]) + (wide[64:96] + wide[96:128])


def wall_loads(load, pick, metric, s, scaled_z, wm):
    wz = mm(pick[128:192], wm[:, 512:768])
    out = []
    for side, sign in ((0, -1.0), (1, 1.0)):
        g = scaled_z[32 * side : 32 * side + 32]
        v = s[128 + 32 * side : 160 + 32 * side]
        parts = [0.2 * sign * g[:, 0:256], 0.2 * sign * g[:, 256:512]]
        w = wz[32 * side : 32 * side + 32]
        parts.append(
            sign * (0.2 * g[:, 512:768] - v[:, 768:1024] + 0.5 * (v[:, 512:768] - w))
        )
        hi, lo = split(jnp.concatenate(parts, 0))
        out.append(table_times(load, hi, lo))
    return jnp.concatenate(out, 1)


MESH = pl.DeviceIdType.MESH


def is_fluid():
    return lax.axis_index("grp") < FLUID


def at(grp, gx, gy):
    return dict(device_id=(grp, gx, gy), device_id_type=MESH)


def store_rows(ref, value):
    for o in range(ref.shape[0]):
        ref[o] = value[4 * o : 4 * o + 4, :]


def load_rows(ref):
    return jnp.concatenate([ref[o] for o in range(ref.shape[0])], 0)


def solid_tables(k):
    r, c = iota((128, 128), 0), iota((128, 128), 1)
    eye = r == c
    diag = jnp.where(eye, k, 0.0)
    col = jnp.sum(diag, 1, keepdims=True)
    row = jnp.sum(diag, 0, keepdims=True)
    one = jnp.where(eye, 1.0, 0.0)
    s = one - RELAX * k / col
    s2 = mm_full(s, s)
    s4 = mm_full(s2, s2)
    t = mm_full(one + s, one + s2) * (RELAX / row)
    sel = jnp.where((c == 3 * (r & 31) + 2) & ((r & 31) < 27), 1.0, 0.0)
    load = mm_full(t, sel.T)
    top = mm_full(sel, load).T
    return s4, load, top


def strided(ref, a):
    return ref[pl.ds(a, 81, stride=32), :]


def top_sources(wide, disp, modulus, pow_):
    r, c = iota((32, 81), 0), iota((32, 81), 1)
    sel = as_bf16((c == 3 * r + 2) & (r < 27))
    r, c = iota((32, 128), 0), iota((32, 128), 1)
    sel_wide = jnp.where((c == 3 * r + 2) & (r < 27), 1.0, 0.0)
    ph, plo = split(mm_full(sel_wide, pow_)[:, 0:81])
    for k in range(16):
        cols = slice(256 * k, 256 * k + 256)
        d = jnp.concatenate([strided(disp, 2 * k), strided(disp, 2 * k + 1)], 1)
        dh, dl = split(d)
        base = mm(ph, dh) + (mm(ph, dl) + mm(plo, dh))
        inv = jnp.broadcast_to(1.0 / modulus[:, cols], (32, 256))
        bh, bl = split(jnp.where(iota((32, 256), 0) == 27, inv, base))
        wide[0:32, cols] = bh
        wide[32:64, cols] = bl
        wide[64:96, cols] = mm(sel, dh).astype(BF16)
        wide[96:128, cols] = mm(sel, dl).astype(BF16)


def target_row(targets):
    turned = targets.T
    return jnp.concatenate([turned[32 * q : 32 * q + 1, :] for q in range(4)], 1).astype(I32) - 1


def stack_slots(x):
    return jnp.concatenate([x[:, 384 * q : 384 * q + 384] for q in range(4)], 0).T


def gather_top(acc, wide, row):
    high = row >> 7
    low = as_bf16(iota((128, 1536), 0) == (row & 127))
    acc[...] = jnp.zeros((128, 1536), F32)

    def step(i, carry):
        parts = [low * as_bf16(high == 4 * i + j) for j in range(4)]
        one = jnp.concatenate(parts, 0)
        acc[...] += mm(wide[:, pl.ds(pl.multiple_of(512 * i, 512), 512)], one)
        return carry
    lax.fori_loop(0, 8, step, 0)
    base = acc[0:32, :] + acc[32:64, :]
    disp = acc[64:96, :] + acc[96:128, :]
    inv = jnp.broadcast_to(base[27:28, :], (32, 1536))
    return stack_slots(base), stack_slots(disp), stack_slots(inv)


def window_kernel(
    state, speed, metric, face, owner, target, stiff, volume, slope, pick, inject, load,
    disp_any, modulus,
    next_o, wm_o, meta_o, back_o, back0_o, pow_o, load_o, got_o, tgt_o,
    part, fields, u0_s, sx, sy, rx, ry, tgt_s, pay_s, got_t, got_p, rows_s, disp_s, back, back0,
    disp, wide, acc, same, gathered, square,
    hs, hr, bs, br, cs,
):
    grp, gx, gy = lax.axis_index("grp"), lax.axis_index("gx"), lax.axis_index("gy")
    fluid = grp < FLUID
    barrier = pltpu.get_barrier_semaphore()
    column = gx * GY + gy
    has = [gx > 0, gx < GX - 1, gy > 0, gy < GY - 1]
    where = [(grp, gx - 1, gy), (grp, gx + 1, gy), (grp, gx, gy - 1), (grp, gx, gy + 1)]
    owner_group = FLUID + lax.rem(grp, SOLID)
    my_row = (grp // SOLID) * COLS + column

    def halo(stage, k, side):
        buf, into = ((sx, rx), (sy, ry))[k // 2]
        return pltpu.make_async_remote_copy(
            buf.at[stage, k % 2], into.at[stage, side % 2], hs.at[stage, k], hr.at[stage, side],
            **at(*where[k]),
        )

    def start_halos(stage):
        for k in range(4):
            @pl.when(has[k])
            def _():
                halo(stage, k, k ^ 1).start()

    def wait_halos(stage):
        for k in range(4):
            @pl.when(has[k])
            def _():
                halo(stage, k, k).wait_recv()

    def far_faces(stage):
        zero = jnp.zeros((), F32)
        return remote_faces(
            jnp.where(has[0], rx[stage, 0], zero), jnp.where(has[1], rx[stage, 1], zero),
            jnp.where(has[2], ry[stage, 0], zero), jnp.where(has[3], ry[stage, 1], zero),
        )

    def push_to_solid(src, dst, k):
        def push(i, carry):
            o = lax.rem(i + column, COLS)
            pltpu.make_async_remote_copy(
                src.at[o], dst.at[my_row], bs.at[k], br.at[k],
                **at(owner_group, o // GY, lax.rem(o, GY)),
            ).start()
            return carry
        lax.fori_loop(0, COLS, push, 0)

    def push_to_fluid(src, dst, k):
        def push(i, carry):
            level = lax.rem(i, LEVELS)
            c = lax.rem(i // LEVELS + column, COLS)
            pltpu.make_async_remote_copy(
                src.at[level * COLS + c], dst.at[column], bs.at[k], br.at[k],
                **at(level * SOLID + (grp - FLUID), c // GY, lax.rem(c, GY)),
            ).start()
            return carry
        lax.fori_loop(0, LEVELS * COLS, push, 0)

    def whole(ref, k):
        return pltpu.make_async_remote_copy(
            ref, ref, bs.at[k], br.at[k], **at(lax.rem(grp + 1, FLUID + SOLID), gx, gy)
        )

    @pl.when(fluid)
    def _():
        peers = jnp.int32(COLS)
        for k in range(4):
            peers = peers + jnp.where(has[k], 1, 0)

            @pl.when(has[k])
            def _():
                pl.semaphore_signal(barrier, inc=1, **at(*where[k]))

        def greet(i, carry):
            o = lax.rem(i + column, COLS)
            pl.semaphore_signal(barrier, inc=1, **at(owner_group, o // GY, lax.rem(o, GY)))
            return carry
        lax.fori_loop(0, COLS, greet, 0)

        met = flat_metric(metric[...])
        u0 = unpack_nodes(state[...].astype(F32), 4, 250)
        wm = unpack_nodes(speed[...].astype(F32), 3, 256)
        u0_s[...] = u0
        wm_o[...] = wm
        meta = wall_meta(face[...], owner[...])
        meta_o[...] = meta
        plus, minus, _, _ = face_values((pick[...], slope[...]), met, u0, None)
        sx[0, 0], sx[0, 1], sy[0, 0], sy[0, 1] = send_faces(plus, minus)
        store_rows(
            tgt_s, to_slots(meta, jnp.broadcast_to((target[...] + 1).astype(F32), (128, 256)))
        )
        rate = volume_rate(volume[...], met, u0.astype(F32), u0, None, wm)
        faces = local_faces(plus, minus, *open_rows(meta))
        part[...] = rate + inject_faces(inject[...], faces)
        pl.semaphore_wait(barrier, peers)
        start_halos(0)
        push_to_solid(tgt_s, got_t, 0)
        wait_halos(0)

        rate = part[...] + inject_faces(inject[...], far_faces(0))
        v1 = u0_s[...].astype(F32) + DT * rate
        fields[...] = v1
        hi, lo = split(v1)
        plus, minus, s, scaled = face_values((pick[...], slope[...]), met, hi, lo)
        loads = wall_loads(load[...], pick[...], met, s, scaled[2], wm_o[...])
        lh, ll = split(loads)
        hit = as_bf16(iota((512, 256), 0) == face[...])
        rows = mm(lh, hit) + mm(ll, hit)
        store_rows(pay_s, to_slots(meta_o[...], jnp.concatenate([rows] * 4, 0)))
        sx[1, 0], sx[1, 1], sy[1, 0], sy[1, 1] = send_faces(plus, minus)
        push_to_solid(pay_s, got_p, 1)
        start_halos(1)

        faces = local_faces(plus, minus, *open_rows(meta_o[...]))
        rate = volume_rate(volume[...], met, fields[...], hi, lo, wm_o[...])
        part[...] = rate
        wait_halos(1)
        faces = [a + b for a, b in zip(faces[:4], far_faces(1))] + faces[4:]
        rate = part[...] + inject_faces(inject[...], faces)
        result = 0.5 * (u0_s[...].astype(F32) + fields[...]) + (0.5 * DT) * rate
        next_o[...] = result.astype(BF16)
        for stage in range(2):
            for k in range(4):
                @pl.when(has[k])
                def _():
                    halo(stage, k, k ^ 1).wait_send()
        whole(tgt_s, 0).wait_send()
        whole(pay_s, 1).wait_send()
        whole(back0, 2).wait_recv()
        back0_o[...] = load_rows(back0)
        whole(back, 3).wait_recv()
        back_o[...] = load_rows(back)

    @pl.when(jnp.logical_not(fluid))
    def _():
        copy = pltpu.make_async_copy(disp_any, disp, cs)
        copy.start()

        def greet(i, carry):
            g = lax.rem(i, LEVELS) * SOLID + (grp - FLUID)
            c = lax.rem(i // LEVELS + column, COLS)
            pl.semaphore_signal(barrier, inc=1, **at(g, c // GY, lax.rem(c, GY)))
            return carry
        lax.fori_loop(0, LEVELS * COLS, greet, 0)

        r, c = iota((128, 128), 0), iota((128, 128), 1)
        square[...] = jnp.where(r == c, 1.0, 0.0)
        square[0:81, 0:81] = stiff[...]
        pow_, load_t, top = solid_tables(square[...])
        pow_o[...] = pow_
        load_o[...] = load_t
        copy.wait()
        top_sources(wide, disp, modulus, pow_)
        th, tl = split(top)
        pl.semaphore_wait(barrier, LEVELS * COLS)

        whole(got_t, 0).wait_recv()
        targets = load_rows(got_t)
        tgt_o[...] = targets
        row = target_row(targets)
        base, d0, inv = gather_top(acc, wide, row)
        store_rows(disp_s, d0)
        wanted = targets.astype(I32) - 1
        for q in range(4):
            same[384 * q : 384 * q + 384, :] = as_bf16(wanted[:, 32 * q : 32 * q + 1] == row)
        push_to_fluid(disp_s, back0, 2)

        whole(got_p, 1).wait_recv()
        loads = load_rows(got_p)
        got_o[...] = loads
        lane = iota((384, 128), 1)
        for q in range(4):
            h, l = split(jnp.where((lane >> 5) == q, loads, 0.0))
            gathered[384 * q : 384 * q + 384, 0:128] = h
            gathered[384 * q : 384 * q + 384, 128:256] = l
        total = jnp.zeros((384, 128), F32)
        for q in range(4):
            both = mm(same[384 * q : 384 * q + 384, :], gathered[...])
            ah, al = split(both[:, 0:128] + both[:, 128:256])
            res = mm(ah, th) + (mm(al, th) + mm(ah, tl))
            total = jnp.where((lane >> 5) == q, res, total)
        store_rows(rows_s, base + inv * total)
        push_to_fluid(rows_s, back, 3)
        whole(disp_s, 2).wait_send()
        whole(rows_s, 3).wait_send()


def final_kernel(
    dn, d0, meta_r, face, wm, blend, nxt,
    disp_any, modulus, pow_, load, pay, tgt,
    next_o, motion_o, solid_o,
    disp, stage, sem,
):
    r, c = iota((256, 256), 0), iota((256, 256), 1)

    @pl.when(is_fluid())
    def _():
        solid_o[...] = jnp.zeros((2592, 128), F32)
        stage[...] = jnp.zeros((1000, 128), F32)
        result = nxt[...]
        for f in range(4):
            at_row = r - 2 * f
            put = as_bf16(
                (at_row >= 0) & (at_row < 250) & (c == (at_row >> 1) + 128 * (at_row & 1))
            )
            block = result[:, 256 * f : 256 * f + 256]
            pair = jnp.concatenate([block[:, 0:128], block[:, 128:256]], 0)
            stage[248 * f : 248 * f + 256, :] = stage[248 * f : 248 * f + 256, :] + mm(put, pair)
        next_o[...] = stage[...].astype(BF16)

        meta = meta_r[...]
        a = from_slots(meta, dn[...])
        b = from_slots(meta, d0[...])
        hi, lo = split(jnp.concatenate([a, a - b], 0))
        hit = as_bf16(iota((512, 256), 0) == face[...])
        faces = mm_nt(hi, hit) + mm_nt(lo, hit)
        faces = jnp.concatenate([faces[:, 0:256], faces[:, 256:512]], 0)
        hi, lo = split(faces)
        put = as_bf16(c == (r >> 1) + 128 * (r & 1))
        for ch in range(6):
            value = table_times(blend[128 * ch : 128 * ch + 128, :], hi, lo)
            if ch >= 3:
                value = value + wm[:, 256 * (ch - 3) : 256 * (ch - 3) + 256].astype(F32)
            value = value.astype(BF16)
            pair = jnp.concatenate([value[:, 0:128], value[:, 128:256]], 0)
            motion_o[256 * ch : 256 * ch + 256, :] = mm(put, pair).astype(BF16)

    @pl.when(jnp.logical_not(is_fluid()))
    def _():
        copy = pltpu.make_async_copy(disp_any, disp, sem)
        copy.start()
        next_o[...] = jnp.zeros((1000, 128), BF16)
        motion_o[...] = jnp.zeros((1536, 128), BF16)
        row = target_row(tgt[...])
        high = row >> 7
        low = as_bf16(iota((128, 1536), 0) == (row & 127))
        turned = pay[...].T
        wide = jnp.concatenate([turned[32 * q : 32 * q + 32, :] for q in range(4)], 1)
        hi, lo = split(wide)
        th, tl = split(load[...][0:81, 0:32])
        sh, sl = split(pow_[...][0:81, 0:81])
        copy.wait()
        for k in range(8):
            masks = [as_bf16(high == 4 * k + j) for j in range(4)]
            parts = [part * mask for mask in masks for part in (hi, lo)]
            force = mm_nt(jnp.concatenate(parts, 0), low)
            for pair in range(2):
                f = [
                    force[64 * j : 64 * j + 32] + force[64 * j + 32 : 64 * j + 64]
                    for j in (2 * pair, 2 * pair + 1)
                ]
                block = 2 * k + pair
                cols = slice(256 * block, 256 * block + 256)
                fh, fl = split(jnp.concatenate(f, 1) / modulus[:, cols])
                d = jnp.concatenate([strided(disp, 2 * block), strided(disp, 2 * block + 1)], 1)
                dh, dl = split(d)
                out = mm(sh, dh) + (mm(sh, dl) + mm(sl, dh))
                out = out + (mm(th, fh) + (mm(th, fl) + mm(tl, fh)))
                solid_o[pl.ds(2 * block, 81, stride=32), :] = out[:, 0:128]
                solid_o[pl.ds(2 * block + 1, 81, stride=32), :] = out[:, 128:256]


VM = pl.BlockSpec(memory_space=pltpu.VMEM)
ANY = pl.BlockSpec(memory_space=pl.ANY)


def shape(dims, dtype=F32):
    return jax.ShapeDtypeStruct(dims, dtype)


def local(
    fluid_state, mesh_velocity, metric, wall_face, wall_owner, wall_target, solid_disp, modulus,
    stiffness,
):
    tab = {k: jnp.asarray(v) for k, v in build_tables().items()}
    state = fluid_state.reshape(1000, 128)
    speed = jnp.pad(
        mesh_velocity.reshape(3, 125, 2, 128), ((0, 0), (0, 3), (0, 0), (0, 0))
    ).reshape(768, 128)
    met = metric.reshape(3, 2, 128)
    face = wall_face.reshape(1, 256)
    owner = wall_owner.reshape(1, 256)
    target = wall_target.reshape(1, 256)
    disp = solid_disp.reshape(2592, 128)
    mod = modulus.reshape(1, 4096)
    slots = LEVELS * COLS

    nxt, wm, meta, back, back0, pow_, load, got_p, got_t = pl.pallas_call(
        window_kernel,
        out_shape=[
            shape((128, 1024), BF16), shape((128, 768), BF16), shape((8, 256)),
            shape((128, 128)), shape((128, 128)), shape((128, 128)), shape((128, 128)),
            shape((384, 128)), shape((384, 128)),
        ],
        in_specs=[VM] * 12 + [ANY, VM],
        out_specs=[VM] * 9,
        scratch_shapes=[
            pltpu.VMEM((128, 1024), F32), pltpu.VMEM((128, 1024), F32),
            pltpu.VMEM((128, 1024), BF16),
            pltpu.VMEM((2, 2, 32, 1024), F32), pltpu.VMEM((2, 2, 32, 512), F32),
            pltpu.VMEM((2, 2, 32, 1024), F32), pltpu.VMEM((2, 2, 32, 512), F32),
            pltpu.VMEM((COLS, 4, 128), F32), pltpu.VMEM((COLS, 4, 128), F32),
            pltpu.VMEM((slots, 4, 128), F32), pltpu.VMEM((slots, 4, 128), F32),
            pltpu.VMEM((slots, 4, 128), F32), pltpu.VMEM((slots, 4, 128), F32),
            pltpu.VMEM((COLS, 4, 128), F32), pltpu.VMEM((COLS, 4, 128), F32),
            pltpu.VMEM((2592, 128), F32), pltpu.VMEM((128, 4096), BF16),
            pltpu.VMEM((128, 1536), F32), pltpu.VMEM((1536, 1536), BF16),
            pltpu.VMEM((1536, 256), BF16), pltpu.VMEM((128, 128), F32),
            pltpu.SemaphoreType.DMA((2, 4)), pltpu.SemaphoreType.DMA((2, 4)),
            pltpu.SemaphoreType.DMA((4,)), pltpu.SemaphoreType.DMA((4,)),
            pltpu.SemaphoreType.DMA,
        ],
        compiler_params=pltpu.CompilerParams(
            collective_id=0, has_side_effects=True, vmem_limit_bytes=60 * 1024 * 1024
        ),
        name="window",
    )(state, speed, met, face, owner, target, stiffness, tab["volume"], tab["slope"], tab["pick"],
      tab["inject"], tab["load"], disp, mod)

    fluid_next, motion, solid_next = pl.pallas_call(
        final_kernel,
        out_shape=[shape((1000, 128), BF16), shape((1536, 128), BF16), shape((2592, 128))],
        in_specs=[VM] * 7 + [ANY] + [VM] * 5,
        out_specs=[VM] * 3,
        scratch_shapes=[
            pltpu.VMEM((2592, 128), F32), pltpu.VMEM((1000, 128), F32), pltpu.SemaphoreType.DMA,
        ],
        compiler_params=pltpu.CompilerParams(vmem_limit_bytes=60 * 1024 * 1024),
        name="final",
    )(back, back0, meta, face, wm, tab["blend"], nxt, disp, mod, pow_, load, got_p, got_t)

    motion = motion.reshape(6, 128, 2, 128)[:, 0:125]
    return (
        fluid_next.reshape(1, 4, 125, 1, 2, 128),
        motion.reshape(1, 6, 125, 1, 2, 128),
        solid_next.reshape(1, 81, 4096),
    )


def solution(mesh):
    in_specs = (
        P("grp", None, None, "gx", "gy", None),
        P("grp", None, None, "gx", "gy", None),
        P("grp", None, "gx", "gy", None),
        P(("grp", "gx", "gy")),
        P(("grp", "gx", "gy"), None),
        P(("grp", "gx", "gy")),
        P("grp", None, ("gx", "gy")),
        P("grp", ("gx", "gy")),
        P(),
    )
    out_specs = (
        P("grp", None, None, "gx", "gy", None),
        P("grp", None, None, "gx", "gy", None),
        P("grp", None, ("gx", "gy")),
    )
    return jax.shard_map(local, mesh=mesh, in_specs=in_specs, out_specs=out_specs, check_vma=False)
```

time: 86.3 us -> 52.6 us (0.61); the launches traced: 84.7 us -> 52.4 us
  Pallas kernels: 72.2 us -> 48 us
  local copies, waits for them, and re-layouts: 10.3 us -> 3.76 us
  other arithmetic: 1.48 us -> 0 us
    pallas_call x7 -> x2, Pallas kernels: 72.2 us -> 48 us  [the longest x1 43.7 us: local(): pl.pallas_call(window_kernel, out_shape=[shape((128, 1024), BF16), shape(...]
    unnamed x7 -> x0, local copies, waits for them, and re-layouts: 5.8 us -> none
    reshape x3 -> x1, local copies, waits for them, and re-layouts: 3.84 us -> 2 us  [local(): motion.reshape(1, 6, 125, 1, 2, 128)]
    add x1 -> x0, other arithmetic: 1.48 us -> none  [local(): jnp.pad(stiffness, ((0, 47), (0, 47)))]
    pad x1, local copies, waits for them, and re-layouts: 0.69 us -> 1.76 us  [local(): jnp.pad(mesh_velocity.reshape(3, 125, 2, 128), ((0, 0), (0, 3), (0, 0), (...]
where the time goes in v1:
time: 52.6 us; the launch traced here: 52.4 us
  Pallas kernels  48 us (91%)
  local copies, waits for them, and re-layouts  3.76 us (7%)
  between operations  0.65 us (1%)
    pallas_call x1, Pallas kernels, local(): pl.pallas_call(window_kernel, out_shape=[shape((128, 1024), BF16), shape(...  43.7 us
    pallas_call x1, Pallas kernels, local(): pl.pallas_call(final_kernel, out_shape=[shape((1000, 128), BF16), shape((...  4.27 us
    reshape x1, local copies, waits for them, and re-layouts, local(): motion.reshape(1, 6, 125, 1, 2, 128)  2 us
    pad x1, local copies, waits for them, and re-layouts, local(): jnp.pad(mesh_velocity.reshape(3, 125, 2, 128), ((0, 0), (0, 3), (0, 0), (...  1.76 us

profile of v1, /device:TPU:1, one launch (start us, length us, event | category | flops | bytes accessed | tf_op | source)
XLA Modules:
  0.0 52.4 jit_solution(7035559988750656097)
XLA Ops:
  0.6 1.8 %pad.4 = bf16[3,128,2,128]{3,2,1,0:T(2,128)(2,1)} pad(bf16[3,125,2,128]{3,2,1,0:T(2,128)(2,1)} %bitcast.20, bf16[]{:T(256)} %constant.14.clone.1), padding=0_0x0_3x0_0x0_0 | pad | bytes 388610 | tf_op jit(solution)/shard_map/jit(_pad)/pad | solution.py:696
  2.4 43.7 %window.1 = (bf16[128,1024]{1,0:T(8,128)(2,1)}, bf16[128,768]{1,0:T(8,128)(2,1)}, f32[8,256]{1,0:T(8,128)}, f32[128,128]{1,0:T(8,128)}, f32[128,128]{1,0:T(8,128...) custom-call(bf16[1000,128]{1,0:T(8,128)(2,1)} %bitcast.19, ...), custom_call_target="tpu_custom_call" | custom-call | tf_op jit(solution)/shard_map/window/pallas_call | solution.py:707
  46.1 4.3 %final.1 = (bf16[1000,128]{1,0:T(8,128)(2,1)}, bf16[1536,128]{1,0:T(8,128)(2,1)}, f32[2592,128]{1,0:T(8,128)}) custom-call(f32[128,128]{1,0:T(8,128)} %get-tuple-element.15.dn, f32[128,128]{1,0:T(8,128)} %get-tuple-element.16.d0, f32[8,256]{1,0:T(8,128)} %get-tuple-element.17.meta_r, s32[1,256]{1,0:T(1,128)} %bitcast.22, ...), custom_call_target="tpu_custom_call" | custom-call | tf_op jit(solution)/shard_map/final/pallas_call | solution.py:739
  50.4 2.0 %slice_bitcast_fusion = bf16[1,6,125,1,2,128]{5,4,3,2,1,0:T(2,128)(2,1)} fusion(bf16[6,128,2,128]{3,2,1,0:T(2,128)(2,1)} %bitcast.18), kind=kLoop, calls=%fused_computation | loop fusion | bytes 768000 | tf_op jit(solution)/shard_map/reshape | solution.py:754

commit v2 on v1

--- a/solution.py
+++ b/solution.py
@@ -358,29 +358,42 @@
     t = mm_full(one + s, one + s2) * (RELAX / row)
     sel = jnp.where((c == 3 * (r & 31) + 2) & ((r & 31) < 27), 1.0, 0.0)
     load = mm_full(t, sel.T)
-    top = mm_full(sel, load).T
+    top = mm_full(sel[0:32], load)[:, 0:32]
     return s4, load, top
+
+
+def pack_pairs(stage, f, pair):
+    start = 250 * f // 8 * 8
+    r, c = iota((256, 256), 0), iota((256, 256), 1)
+    at_row = r - (250 * f - start)
+    put = as_bf16((at_row >= 0) & (at_row < 250) & (c == (at_row >> 1) + 128 * (at_row & 1)))
+    value = mm(put, pair)
+    if 250 * f % 8:
+        stage[start : start + 8, :] = stage[start : start + 8, :] + value[0:8]
+        stage[start + 8 : start + 256, :] = value[8:256]
+    else:
+        stage[start : start + 256, :] = value
 
 
 def strided(ref, a):
     return ref[pl.ds(a, 81, stride=32), :]
 
 
-def top_sources(wide, disp, modulus, pow_):
+def power_sources(keep, wide, disp, modulus, pow_):
     r, c = iota((32, 81), 0), iota((32, 81), 1)
     sel = as_bf16((c == 3 * r + 2) & (r < 27))
-    r, c = iota((32, 128), 0), iota((32, 128), 1)
-    sel_wide = jnp.where((c == 3 * r + 2) & (r < 27), 1.0, 0.0)
-    ph, plo = split(mm_full(sel_wide, pow_)[:, 0:81])
+    ph, plo = split(pow_[0:81, 0:81])
     for k in range(16):
         cols = slice(256 * k, 256 * k + 256)
         d = jnp.concatenate([strided(disp, 2 * k), strided(disp, 2 * k + 1)], 1)
         dh, dl = split(d)
-        base = mm(ph, dh) + (mm(ph, dl) + mm(plo, dh))
-        inv = jnp.broadcast_to(1.0 / modulus[:, cols], (32, 256))
-        bh, bl = split(jnp.where(iota((32, 256), 0) == 27, inv, base))
-        wide[0:32, cols] = bh
-        wide[32:64, cols] = bl
+        value = mm(ph, dh) + (mm(ph, dl) + mm(plo, dh))
+        keep[:, cols] = value
+        kh, kl = split(value)
+        inv_h, inv_l = split(jnp.broadcast_to(1.0 / modulus[:, cols], (32, 256)))
+        spare = iota((32, 256), 0) == 27
+        wide[0:32, cols] = jnp.where(spare, inv_h.astype(F32), mm(sel, kh)).astype(BF16)
+        wide[32:64, cols] = jnp.where(spare, inv_l.astype(F32), mm(sel, kl)).astype(BF16)
         wide[64:96, cols] = mm(sel, dh).astype(BF16)
         wide[96:128, cols] = mm(sel, dl).astype(BF16)
 
@@ -405,18 +418,15 @@
         acc[...] += mm(wide[:, pl.ds(pl.multiple_of(512 * i, 512), 512)], one)
         return carry
     lax.fori_loop(0, 8, step, 0)
-    base = acc[0:32, :] + acc[32:64, :]
-    disp = acc[64:96, :] + acc[96:128, :]
-    inv = jnp.broadcast_to(base[27:28, :], (32, 1536))
-    return stack_slots(base), stack_slots(disp), stack_slots(inv)
+    return acc[0:32, :] + acc[32:64, :], acc[64:96, :] + acc[96:128, :]
 
 
 def window_kernel(
     state, speed, metric, face, owner, target, stiff, volume, slope, pick, inject, load,
     disp_any, modulus,
-    next_o, wm_o, meta_o, back_o, back0_o, pow_o, load_o, got_o, tgt_o,
+    next_o, wm_o, meta_o, back_o, back0_o, solid_o,
     part, fields, u0_s, sx, sy, rx, ry, tgt_s, pay_s, got_t, got_p, rows_s, disp_s, back, back0,
-    disp, wide, acc, same, gathered, square,
+    disp, wide, acc, same, keep, square, raw, stage_s,
     hs, hr, bs, br, cs,
 ):
     grp, gx, gy = lax.axis_index("grp"), lax.axis_index("gx"), lax.axis_index("gy")
@@ -454,26 +464,29 @@
             jnp.where(has[2], ry[stage, 0], zero), jnp.where(has[3], ry[stage, 1], zero),
         )
 
+    others = [lax.rem(gy + b, GY) for b in range(GY)]
+
     def push_to_solid(src, dst, k):
         def push(i, carry):
-            o = lax.rem(i + column, COLS)
-            pltpu.make_async_remote_copy(
-                src.at[o], dst.at[my_row], bs.at[k], br.at[k],
-                **at(owner_group, o // GY, lax.rem(o, GY)),
-            ).start()
+            x = lax.rem(gx + i, GX)
+            for y in others:
+                pltpu.make_async_remote_copy(
+                    src.at[x * GY + y], dst.at[my_row], bs.at[k], br.at[k], **at(owner_group, x, y)
+                ).start()
             return carry
-        lax.fori_loop(0, COLS, push, 0)
+        lax.fori_loop(0, GX, push, 0)
 
     def push_to_fluid(src, dst, k):
         def push(i, carry):
-            level = lax.rem(i, LEVELS)
-            c = lax.rem(i // LEVELS + column, COLS)
-            pltpu.make_async_remote_copy(
-                src.at[level * COLS + c], dst.at[column], bs.at[k], br.at[k],
-                **at(level * SOLID + (grp - FLUID), c // GY, lax.rem(c, GY)),
-            ).start()
+            x = lax.rem(gx + i, GX)
+            for level in range(LEVELS):
+                for y in others:
+                    pltpu.make_async_remote_copy(
+                        src.at[level * COLS + x * GY + y], dst.at[column], bs.at[k], br.at[k],
+                        **at(level * SOLID + (grp - FLUID), x, y),
+                    ).start()
             return carry
-        lax.fori_loop(0, LEVELS * COLS, push, 0)
+        lax.fori_loop(0, GX, push, 0)
 
     def whole(ref, k):
         return pltpu.make_async_remote_copy(
@@ -491,14 +504,18 @@
                 pl.semaphore_signal(barrier, inc=1, **at(*where[k]))
 
         def greet(i, carry):
-            o = lax.rem(i + column, COLS)
-            pl.semaphore_signal(barrier, inc=1, **at(owner_group, o // GY, lax.rem(o, GY)))
+            x = lax.rem(gx + i, GX)
+            for y in others:
+                pl.semaphore_signal(barrier, inc=1, **at(owner_group, x, y))
             return carry
-        lax.fori_loop(0, COLS, greet, 0)
+        lax.fori_loop(0, GX, greet, 0)
 
         met = flat_metric(metric[...])
         u0 = unpack_nodes(state[...].astype(F32), 4, 250)
-        wm = unpack_nodes(speed[...].astype(F32), 3, 256)
+        raw[744:752, :] = jnp.zeros((8, 128), F32)
+        for i in range(375):
+            raw[2 * i : 2 * i + 2, :] = speed[i].astype(F32)
+        wm = unpack_nodes(raw[...], 3, 250)
         u0_s[...] = u0
         wm_o[...] = wm
         meta = wall_meta(face[...], owner[...])
@@ -537,7 +554,11 @@
         faces = [a + b for a, b in zip(faces[:4], far_faces(1))] + faces[4:]
         rate = part[...] + inject_faces(inject[...], faces)
         result = 0.5 * (u0_s[...].astype(F32) + fields[...]) + (0.5 * DT) * rate
-        next_o[...] = result.astype(BF16)
+        result = result.astype(BF16)
+        for f in range(4):
+            block = result[:, 256 * f : 256 * f + 256]
+            pack_pairs(stage_s, f, jnp.concatenate([block[:, 0:128], block[:, 128:256]], 0))
+        next_o[...] = stage_s[...].astype(BF16)
         for stage in range(2):
             for k in range(4):
                 @pl.when(has[k])
@@ -556,109 +577,45 @@
         copy.start()
 
         def greet(i, carry):
-            g = lax.rem(i, LEVELS) * SOLID + (grp - FLUID)
-            c = lax.rem(i // LEVELS + column, COLS)
-            pl.semaphore_signal(barrier, inc=1, **at(g, c // GY, lax.rem(c, GY)))
+            x = lax.rem(gx + i, GX)
+            for level in range(LEVELS):
+                for y in others:
+                    pl.semaphore_signal(barrier, inc=1, **at(level * SOLID + (grp - FLUID), x, y))
             return carry
-        lax.fori_loop(0, LEVELS * COLS, greet, 0)
+        lax.fori_loop(0, GX, greet, 0)
 
         r, c = iota((128, 128), 0), iota((128, 128), 1)
         square[...] = jnp.where(r == c, 1.0, 0.0)
         square[0:81, 0:81] = stiff[...]
         pow_, load_t, top = solid_tables(square[...])
-        pow_o[...] = pow_
-        load_o[...] = load_t
         copy.wait()
-        top_sources(wide, disp, modulus, pow_)
+        power_sources(keep, wide, disp, modulus, pow_)
         th, tl = split(top)
         pl.semaphore_wait(barrier, LEVELS * COLS)
 
         whole(got_t, 0).wait_recv()
         targets = load_rows(got_t)
-        tgt_o[...] = targets
         row = target_row(targets)
-        base, d0, inv = gather_top(acc, wide, row)
-        store_rows(disp_s, d0)
+        base, d0 = gather_top(acc, wide, row)
+        store_rows(disp_s, stack_slots(d0))
+        push_to_fluid(disp_s, back0, 2)
         wanted = targets.astype(I32) - 1
         for q in range(4):
             same[384 * q : 384 * q + 384, :] = as_bf16(wanted[:, 32 * q : 32 * q + 1] == row)
-        push_to_fluid(disp_s, back0, 2)
 
         whole(got_p, 1).wait_recv()
-        loads = load_rows(got_p)
-        got_o[...] = loads
-        lane = iota((384, 128), 1)
-        for q in range(4):
-            h, l = split(jnp.where((lane >> 5) == q, loads, 0.0))
-            gathered[384 * q : 384 * q + 384, 0:128] = h
-            gathered[384 * q : 384 * q + 384, 128:256] = l
-        total = jnp.zeros((384, 128), F32)
-        for q in range(4):
-            both = mm(same[384 * q : 384 * q + 384, :], gathered[...])
-            ah, al = split(both[:, 0:128] + both[:, 128:256])
-            res = mm(ah, th) + (mm(al, th) + mm(ah, tl))
-            total = jnp.where((lane >> 5) == q, res, total)
-        store_rows(rows_s, base + inv * total)
+        turned = load_rows(got_p).T
+        loads = jnp.concatenate([turned[32 * q : 32 * q + 32, :] for q in range(4)], 1)
+        hi, lo = split(loads)
+        both = mm(jnp.concatenate([hi, lo], 0), same[...])
+        fh, fl = split(both[0:32] + both[32:64])
+        total = mm(th, fh) + (mm(tl, fh) + mm(th, fl))
+        store_rows(rows_s, stack_slots(base + base[27:28, :] * total))
         push_to_fluid(rows_s, back, 3)
-        whole(disp_s, 2).wait_send()
-        whole(rows_s, 3).wait_send()
-
-
-def final_kernel(
-    dn, d0, meta_r, face, wm, blend, nxt,
-    disp_any, modulus, pow_, load, pay, tgt,
-    next_o, motion_o, solid_o,
-    disp, stage, sem,
-):
-    r, c = iota((256, 256), 0), iota((256, 256), 1)
-
-    @pl.when(is_fluid())
-    def _():
-        solid_o[...] = jnp.zeros((2592, 128), F32)
-        stage[...] = jnp.zeros((1000, 128), F32)
-        result = nxt[...]
-        for f in range(4):
-            at_row = r - 2 * f
-            put = as_bf16(
-                (at_row >= 0) & (at_row < 250) & (c == (at_row >> 1) + 128 * (at_row & 1))
-            )
-            block = result[:, 256 * f : 256 * f + 256]
-            pair = jnp.concatenate([block[:, 0:128], block[:, 128:256]], 0)
-            stage[248 * f : 248 * f + 256, :] = stage[248 * f : 248 * f + 256, :] + mm(put, pair)
-        next_o[...] = stage[...].astype(BF16)
-
-        meta = meta_r[...]
-        a = from_slots(meta, dn[...])
-        b = from_slots(meta, d0[...])
-        hi, lo = split(jnp.concatenate([a, a - b], 0))
-        hit = as_bf16(iota((512, 256), 0) == face[...])
-        faces = mm_nt(hi, hit) + mm_nt(lo, hit)
-        faces = jnp.concatenate([faces[:, 0:256], faces[:, 256:512]], 0)
-        hi, lo = split(faces)
-        put = as_bf16(c == (r >> 1) + 128 * (r & 1))
-        for ch in range(6):
-            value = table_times(blend[128 * ch : 128 * ch + 128, :], hi, lo)
-            if ch >= 3:
-                value = value + wm[:, 256 * (ch - 3) : 256 * (ch - 3) + 256].astype(F32)
-            value = value.astype(BF16)
-            pair = jnp.concatenate([value[:, 0:128], value[:, 128:256]], 0)
-            motion_o[256 * ch : 256 * ch + 256, :] = mm(put, pair).astype(BF16)
-
-    @pl.when(jnp.logical_not(is_fluid()))
-    def _():
-        copy = pltpu.make_async_copy(disp_any, disp, sem)
-        copy.start()
-        next_o[...] = jnp.zeros((1000, 128), BF16)
-        motion_o[...] = jnp.zeros((1536, 128), BF16)
-        row = target_row(tgt[...])
+
         high = row >> 7
         low = as_bf16(iota((128, 1536), 0) == (row & 127))
-        turned = pay[...].T
-        wide = jnp.concatenate([turned[32 * q : 32 * q + 32, :] for q in range(4)], 1)
-        hi, lo = split(wide)
-        th, tl = split(load[...][0:81, 0:32])
-        sh, sl = split(pow_[...][0:81, 0:81])
-        copy.wait()
+        lh, ll = split(load_t[0:81, 0:32])
         for k in range(8):
             masks = [as_bf16(high == 4 * k + j) for j in range(4)]
             parts = [part * mask for mask in masks for part in (hi, lo)]
@@ -671,12 +628,79 @@
                 block = 2 * k + pair
                 cols = slice(256 * block, 256 * block + 256)
                 fh, fl = split(jnp.concatenate(f, 1) / modulus[:, cols])
-                d = jnp.concatenate([strided(disp, 2 * block), strided(disp, 2 * block + 1)], 1)
-                dh, dl = split(d)
-                out = mm(sh, dh) + (mm(sh, dl) + mm(sl, dh))
-                out = out + (mm(th, fh) + (mm(th, fl) + mm(tl, fh)))
-                solid_o[pl.ds(2 * block, 81, stride=32), :] = out[:, 0:128]
-                solid_o[pl.ds(2 * block + 1, 81, stride=32), :] = out[:, 128:256]
+                out = keep[:, cols] + (mm(lh, fh) + (mm(lh, fl) + mm(ll, fh)))
+                disp[pl.ds(2 * block, 81, stride=32), :] = out[:, 0:128]
+                disp[pl.ds(2 * block + 1, 81, stride=32), :] = out[:, 128:256]
+        copy = pltpu.make_async_copy(disp, solid_o, cs)
+        copy.start()
+        copy.wait()
+        whole(disp_s, 2).wait_send()
+        whole(rows_s, 3).wait_send()
+
+
+def final_kernel(
+    dn, d0, meta_r, face, wm, blend, next_any, solid_any,
+    next_o, motion_o, solid_o,
+    moved, kept, stage, sems,
+):
+    parts = 4
+    size = 2592 // parts
+    next_in = pltpu.make_async_copy(next_any, kept, sems.at[0])
+    next_out = pltpu.make_async_copy(kept, next_o, sems.at[1])
+    ins = [
+        pltpu.make_async_copy(
+            solid_any.at[pl.ds(size * i, size)], moved.at[pl.ds(size * i, size)], sems.at[2 + i]
+        )
+        for i in range(parts)
+    ]
+    outs = [
+        pltpu.make_async_copy(
+            moved.at[pl.ds(size * i, size)], solid_o.at[pl.ds(size * i, size)], sems.at[6 + i]
+        )
+        for i in range(parts)
+    ]
+
+    @pl.when(is_fluid())
+    def _():
+        next_in.start()
+        moved[...] = jnp.zeros((2592, 128), F32)
+        for copy in outs:
+            copy.start()
+        meta = meta_r[...]
+        a = from_slots(meta, dn[...])
+        b = from_slots(meta, d0[...])
+        hi, lo = split(jnp.concatenate([a, a - b], 0))
+        hit = as_bf16(iota((512, 256), 0) == face[...])
+        faces = mm_nt(hi, hit) + mm_nt(lo, hit)
+        faces = jnp.concatenate([faces[:, 0:256], faces[:, 256:512]], 0)
+        hi, lo = split(faces)
+        next_in.wait()
+        next_out.start()
+        for ch in range(6):
+            value = table_times(blend[128 * ch : 128 * ch + 128, :], hi, lo)
+            if ch >= 3:
+                value = value + wm[:, 256 * (ch - 3) : 256 * (ch - 3) + 256].astype(F32)
+            value = value.astype(BF16)
+            pack_pairs(stage, ch, jnp.concatenate([value[:, 0:128], value[:, 128:256]], 0))
+        for i in range(375):
+            motion_o[i] = stage[4 * i : 4 * i + 4, :].astype(BF16)
+        for copy in outs:
+            copy.wait()
+        next_out.wait()
+
+    @pl.when(jnp.logical_not(is_fluid()))
+    def _():
+        for copy in ins:
+            copy.start()
+        kept[...] = jnp.zeros((1000, 128), BF16)
+        next_out.start()
+        motion_o[...] = jnp.zeros((375, 4, 128), BF16)
+        for i in range(parts):
+            ins[i].wait()
+            outs[i].start()
+        for copy in outs:
+            copy.wait()
+        next_out.wait()
 
 
 VM = pl.BlockSpec(memory_space=pltpu.VMEM)
@@ -693,9 +717,7 @@
 ):
     tab = {k: jnp.asarray(v) for k, v in build_tables().items()}
     state = fluid_state.reshape(1000, 128)
-    speed = jnp.pad(
-        mesh_velocity.reshape(3, 125, 2, 128), ((0, 0), (0, 3), (0, 0), (0, 0))
-    ).reshape(768, 128)
+    speed = mesh_velocity.reshape(375, 2, 128)
     met = metric.reshape(3, 2, 128)
     face = wall_face.reshape(1, 256)
     owner = wall_owner.reshape(1, 256)
@@ -704,15 +726,14 @@
     mod = modulus.reshape(1, 4096)
     slots = LEVELS * COLS
 
-    nxt, wm, meta, back, back0, pow_, load, got_p, got_t = pl.pallas_call(
+    nxt, wm, meta, back, back0, moved = pl.pallas_call(
         window_kernel,
         out_shape=[
-            shape((128, 1024), BF16), shape((128, 768), BF16), shape((8, 256)),
-            shape((128, 128)), shape((128, 128)), shape((128, 128)), shape((128, 128)),
-            shape((384, 128)), shape((384, 128)),
+            shape((1000, 128), BF16), shape((128, 768), BF16), shape((8, 256)),
+            shape((128, 128)), shape((128, 128)), shape((2592, 128)),
         ],
         in_specs=[VM] * 12 + [ANY, VM],
-        out_specs=[VM] * 9,
+        out_specs=[VM] * 5 + [ANY],
         scratch_shapes=[
             pltpu.VMEM((128, 1024), F32), pltpu.VMEM((128, 1024), F32),
             pltpu.VMEM((128, 1024), BF16),
@@ -724,7 +745,8 @@
             pltpu.VMEM((COLS, 4, 128), F32), pltpu.VMEM((COLS, 4, 128), F32),
             pltpu.VMEM((2592, 128), F32), pltpu.VMEM((128, 4096), BF16),
             pltpu.VMEM((128, 1536), F32), pltpu.VMEM((1536, 1536), BF16),
-            pltpu.VMEM((1536, 256), BF16), pltpu.VMEM((128, 128), F32),
+            pltpu.VMEM((81, 4096), F32), pltpu.VMEM((128, 128), F32),
+            pltpu.VMEM((752, 128), F32), pltpu.VMEM((1000, 128), F32),
             pltpu.SemaphoreType.DMA((2, 4)), pltpu.SemaphoreType.DMA((2, 4)),
             pltpu.SemaphoreType.DMA((4,)), pltpu.SemaphoreType.DMA((4,)),
             pltpu.SemaphoreType.DMA,
@@ -738,17 +760,17 @@
 
     fluid_next, motion, solid_next = pl.pallas_call(
         final_kernel,
-        out_shape=[shape((1000, 128), BF16), shape((1536, 128), BF16), shape((2592, 128))],
-        in_specs=[VM] * 7 + [ANY] + [VM] * 5,
-        out_specs=[VM] * 3,
+        out_shape=[shape((1000, 128), BF16), shape((375, 4, 128), BF16), shape((2592, 128))],
+        in_specs=[VM] * 6 + [ANY] * 2,
+        out_specs=[ANY, VM, ANY],
         scratch_shapes=[
-            pltpu.VMEM((2592, 128), F32), pltpu.VMEM((1000, 128), F32), pltpu.SemaphoreType.DMA,
+            pltpu.VMEM((2592, 128), F32), pltpu.VMEM((1000, 128), BF16),
+            pltpu.VMEM((1512, 128), F32), pltpu.SemaphoreType.DMA((10,)),
         ],
         compiler_params=pltpu.CompilerParams(vmem_limit_bytes=60 * 1024 * 1024),
         name="final",
-    )(back, back0, meta, face, wm, tab["blend"], nxt, disp, mod, pow_, load, got_p, got_t)
-
-    motion = motion.reshape(6, 128, 2, 128)[:, 0:125]
+    )(back, back0, meta, face, wm, tab["blend"], nxt, moved)
+
     return (
         fluid_next.reshape(1, 4, 125, 1, 2, 128),
         motion.reshape(1, 6, 125, 1, 2, 128),

time: 52.6 us -> 44 us (0.84)
  Pallas kernels: 48 us -> 42.6 us
  local copies, waits for them, and re-layouts: 3.76 us -> 0 us
    pallas_call x1, Pallas kernels: 43.7 us -> 38.7 us  [local(): pl.pallas_call(window_kernel, out_shape=[shape((1000, 128), BF16), shape(...]
    reshape x1 -> x0, local copies, waits for them, and re-layouts: 2 us -> none  [local(): motion.reshape(1, 6, 125, 1, 2, 128)]
    pad x1 -> x0, local copies, waits for them, and re-layouts: 1.76 us -> none  [local(): jnp.pad(mesh_velocity.reshape(3, 125, 2, 128), ((0, 0), (0, 3), (0, 0), (...]
where the time goes in v2:
time: 44 us; the launch traced here: 43.4 us
  Pallas kernels  42.6 us (97%)
  between operations  0.8 us (2%)
    pallas_call x1, Pallas kernels, local(): pl.pallas_call(window_kernel, out_shape=[shape((1000, 128), BF16), shape(...  38.7 us
    pallas_call x1, Pallas kernels, local(): pl.pallas_call(final_kernel, out_shape=[shape((1000, 128), BF16), shape((...  3.88 us

profile of v2, /device:TPU:1, one launch (start us, length us, event | category | flops | bytes accessed | tf_op | source)
XLA Modules:
  0.0 43.4 jit_solution(6643619852288360107)
XLA Ops:
  0.6 38.7 %window.1 = (bf16[1000,128]{1,0:T(8,128)(2,1)}, bf16[128,768]{1,0:T(8,128)(2,1)}, f32[8,256]{1,0:T(8,128)}, f32[128,128]{1,0:T(8,128)}, f32[128,128]{1,0:T(8,128)}, /*index=5*/f32[2592,128]{1,0:T(8,128)}) custom-call(bf16[1000,128]{1,0:T(8,128)(2,1)} %bitcast.15, bf16[375,2,128]{2,1,0:T(2,128)(2,1)} %bitcast.16, f32[3,2,128]{2,1,0:T(2,128)} %bitcast.19, ...), custom_call_target="tpu_custom_call" | custom-call | tf_op jit(solution)/shard_map/window/pallas_call | solution.py:729
  39.4 3.9 %final.1 = (bf16[1000,128]{1,0:T(8,128)(2,1)}, bf16[375,4,128]{2,1,0:T(4,128)(2,1)}, f32[2592,128]{1,0:T(8,128)}) custom-call(f32[128,128]{1,0:T(8,128)} %get-tuple-element.12.dn, f32[128,128]{1,0:T(8,128)} %get-tuple-element.13.d0, f32[8,256]{1,0:T(8,128)} %get-tuple-element.14.meta_r, s32[1,256]{1,0:T(1,128)} %bitcast.18, ...), custom_call_target="tpu_custom_call" | custom-call | tf_op jit(solution)/shard_map/final/pallas_call | solution.py:761
